TPU v7x, 512 devices: a whole 4x4x16 slice. The times are simulated.
512 devices in a mesh: orb: 32 (over x, y, core), pln: 16 (over z).
Axes of the slice: x: 4, y: 4, z: 16, core: 2. Of those that a mesh axis runs over, the one named last changes fastest.
Arguments:
- orbitals: bfloat16 [512, 32768], P('orb'), may hold values from -6 to 6
- occupations: float32 [512], P('orb'), may hold values from 0.5 to 2
- box_offsets: int32 [512, 3], P('orb'), may hold values from 0 to 96
- kernel_spectrum: float32 [256, 256, 256], P(None, 'pln', 'orb'), may hold values from 0.05 to 3.4, as said below
Outputs:
- hartree_terms: bfloat16 [512, 32768], P('orb', 'pln')
Inputs may be any that keep to these rules, and one draw needn't show every extreme that they name: `box_offsets`: each orbital's box of 32 cells a side lies inside the fine grid. `kernel_spectrum`: positive and even: unchanged when any index k is replaced by (256 - k) mod 256.
All inputs are finite; a program needn't handle non-finite values.
Results may differ from a plain program's by a relative error of at most 0.003.
Values may be sent and summed in bfloat16 or wider, within the bound.
A program may use at most 128 MiB of HBM per device.

v0:
```python
import math

import jax
import jax.numpy as jnp
from jax import lax
from jax.sharding import PartitionSpec as P

G = 128
BOX = 32


MAGIC_TAPS = (
    8.433424733352934e-07,
    -1.290557201342061e-05,
    8.76298447621056e-05,
    -0.00030158038132690465,
    0.001747237136729939,
    -0.009420470302010804,
    0.023738214637249424,
    0.0612625895831208,
    0.9940415697834004,
    -0.06048952891969835,
    -0.021030251609303816,
    0.013372634148547948,
    -0.0034412814449349387,
    0.0004944322768868992,
    -5.185986881173433e-05,
    2.7273449291197967e-06,
)
PRECISE = lax.Precision.HIGHEST


def magic_matrix(positions, width):
    taps = jnp.array(MAGIC_TAPS, dtype=jnp.float32)
    shifted = jnp.arange(width, dtype=jnp.int32)[None, :] - positions[:, None]
    hits = (shifted[:, :, None] == jnp.arange(-8, 8, dtype=jnp.int32)[None, None, :]).astype(
        jnp.float32
    )
    inside = ((positions >= 0) & (positions < width)).astype(jnp.float32)
    return jnp.sum(hits * taps, axis=2) * inside[:, None]


def expand_all(coefs, depth_filters, filters):
    section = jnp.einsum("ojk,okyx->ojyx", depth_filters, coefs, precision=PRECISE)
    section = jnp.einsum("ak,ojkx->ojax", filters, section, precision=PRECISE)
    return jnp.einsum("bx,ojax->ojab", filters, section, precision=PRECISE)


def contract_all(weighted, depth_filters, filters):
    section = jnp.einsum("bx,ojab->ojax", filters, weighted, precision=PRECISE)
    section = jnp.einsum("ak,ojax->ojkx", filters, section, precision=PRECISE)
    return jnp.einsum("ojk,ojyx->okyx", depth_filters, section, precision=PRECISE)


def fourier_table(count_in, count_out, doubled, sign):
    inputs = jnp.arange(count_in, dtype=jnp.int32)[:, None]
    outputs = jnp.arange(count_out, dtype=jnp.int32)[None, :]
    phase = inputs * outputs % doubled
    angle = phase.astype(jnp.float32) * (2.0 * math.pi / doubled)
    return (jnp.cos(angle), sign * jnp.sin(angle))


def along(stack, which, tables):
    letters = "abcd"[: stack.ndim - 1]
    target = letters[:which] + "e" + letters[which + 1 :]
    pattern = letters + "," + letters[which] + "e->" + target
    cosine, sine = tables
    real_part = stack[0]
    imag_part = stack[1]

    def multiply(values, table):
        return jnp.einsum(pattern, values, table, precision=PRECISE)

    return jnp.stack(
        [
            multiply(real_part, cosine) - multiply(imag_part, sine),
            multiply(real_part, sine) + multiply(imag_part, cosine),
        ]
    )


def per_device(orbitals, occupations, box_offsets, kernel_spectrum):
    orbital_count = orbitals.shape[0]
    plane_groups = lax.axis_size("pln")
    slab_depth = G // plane_groups
    doubled = 2 * G
    plane_index = lax.axis_index("pln")
    filters = magic_matrix(jnp.arange(BOX, dtype=jnp.int32), BOX)
    coefs = orbitals.astype(jnp.float32).reshape(orbital_count, BOX, BOX, BOX)
    plane_rows = plane_index * slab_depth + jnp.arange(slab_depth, dtype=jnp.int32)
    local_rows = plane_rows[None, :] - box_offsets[:, 0:1]
    depth_filters = jax.vmap(lambda rows: magic_matrix(rows, BOX))(local_rows)
    psi_planes = expand_all(coefs, depth_filters, filters)
    density_terms = occupations[:, None, None, None] * psi_planes * psi_planes
    box_steps = jnp.arange(BOX, dtype=jnp.int32)
    grid_rows = (box_offsets[:, 1:2] + box_steps[None, :])[:, :, None]
    grid_cols = (box_offsets[:, 2:3] + box_steps[None, :])[:, None, :]
    placed_terms = jnp.moveaxis(density_terms, 1, 0)
    partial_density = (
        jnp.zeros((slab_depth, G, G), jnp.float32).at[:, grid_rows, grid_cols].add(placed_terms)
    )
    forward_cos, forward_sin = fourier_table(G, doubled, doubled, -1.0)
    slab = lax.psum_scatter(partial_density, "orb", scatter_dimension=1, tiled=True)
    spectrum = jnp.stack(
        [
            jnp.dot(slab, forward_cos, precision=PRECISE),
            jnp.dot(slab, forward_sin, precision=PRECISE),
        ]
    )
    spectrum = lax.all_to_all(
        spectrum.astype(jnp.bfloat16), "orb", split_axis=3, concat_axis=2, tiled=True
    ).astype(spectrum.dtype)
    spectrum = along(spectrum, 1, (forward_cos, forward_sin))
    spectrum = lax.all_to_all(spectrum, "pln", split_axis=2, concat_axis=1, tiled=True)
    spectrum = along(spectrum, 0, (forward_cos, forward_sin))
    spectrum = spectrum * kernel_spectrum[None]
    inverse_cos, inverse_sin = fourier_table(doubled, G, doubled, 1.0)
    spectrum = along(spectrum, 0, (inverse_cos, inverse_sin))
    spectrum = lax.all_to_all(spectrum, "pln", split_axis=1, concat_axis=2, tiled=True)
    spectrum = along(spectrum, 1, (inverse_cos, inverse_sin))
    spectrum = lax.all_to_all(spectrum, "orb", split_axis=2, concat_axis=3, tiled=True)
    scale = 1.0 / float(doubled) ** 3
    potential_rows = (
        jnp.dot(spectrum[0], inverse_cos, precision=PRECISE)
        - jnp.dot(spectrum[1], inverse_sin, precision=PRECISE)
    ) * scale
    potential_slab = lax.all_gather(potential_rows, "orb", axis=1, tiled=True)
    potential_whole = lax.all_gather(potential_slab, "pln", axis=0, tiled=True)
    own_count = orbital_count // plane_groups
    first = plane_index * own_count
    own_coefs = lax.dynamic_slice_in_dim(coefs, first, own_count, 0)
    own_offsets = lax.dynamic_slice_in_dim(box_offsets, first, own_count, 0)
    full_filters = jnp.broadcast_to(filters, (own_count, BOX, BOX))
    own_psi = expand_all(own_coefs, full_filters, filters)
    own_potential = jax.vmap(
        lambda corner: lax.dynamic_slice(
            potential_whole, (corner[0], corner[1], corner[2]), (BOX, BOX, BOX)
        )
    )(own_offsets)
    finished = (
        contract_all(own_potential * own_psi, full_filters, filters)
        .reshape(own_count, BOX * BOX * BOX)
        .astype(jnp.bfloat16)
    )
    return lax.all_to_all(finished, "pln", split_axis=1, concat_axis=0, tiled=True)


def solution(mesh):
    in_specs = (P("orb", None), P("orb"), P("orb", None), P(None, "pln", "orb"))
    out_specs = P("orb", "pln")
    return jax.shard_map(
        per_device, mesh=mesh, in_specs=in_specs, out_specs=out_specs, check_vma=False
    )
```

profile of v0, /device:TPU:6, one launch (start us, length us, event | category | flops | bytes accessed | tf_op | source)
XLA Modules:
  0.0 495.2 jit_solution(8580559204103528242)
XLA Ops:
  7.5 5.4 %reshape.255 = bf16[16,32,32,32]{3,2,1,0:T(8,128)(2,1)} reshape(bf16[16,32768]{1,0:T(8,128)(2,1)} %param.6) | data formatting | bytes 2097152 | tf_op jit(solution)/shard_map/reshape | solution.py:89
  14.2 5.2 %fusion.67 = f32[16,8,32,32]{3,1,2,0:T(8,128)S(1)} fusion(f32[16,8,32]{2,1,0:T(8,128)S(1)} %select_reduce_fusion, f32[16,8]{1,0:T(8,128)S(1)} %and_convert_fusion, bf16[16,32,32,32]{3,2,1,0:T(8,128)(2,1)} %reshape.255), kind=kOutput, calls=%fused_computation.104 | convolution fusion | flops 50335744 | bytes 1589760 | tf_op jit(solution)/shard_map/ojk,okyx->ojyx/dot_general | solution.py:44
  19.4 3.5 fusion.5
  22.9 3.6 fusion.2
  26.5 5.2 %copy.187 = f32[16,32,32,8]{3,2,1,0:T(8,128)} copy(f32[16,32,32,8]{2,1,3,0:T(8,128)S(1)} %fusion.2) | data formatting | bytes 1048576 | tf_op jit(solution)/shard_map/mul | solution.py:94
  31.8 91.3 %scatter_custom_fusion = f32[8,16384]{0,1:T(8,128)} fusion(s32[16384]{0:T(1024)S(1)} %reshape.294, f32[16384,8]{1,0:T(8,128)} %bitcast.259, f32[]{:T(128)} %constant.19.clone.1), kind=kCustom, calls=%fused_computation.1 | custom fusion | flops 131072 | bytes 524800
  123.1 5.9 %copy.144 = f32[8,128,128]{2,0,1:T(8,128)} copy(f32[8,128,128]{0,2,1:T(8,128)} %bitcast.258) | data formatting | bytes 1048576 | tf_op jit(solution)/shard_map/scatter-add | solution.py:100
  129.0 104.7 %reduce-scatter.2.cloned.1.call-done = f32[8,4,128]{2,0,1:T(8,128)} async-done(((f32[8,128,128]{2,0,1:T(8,128)}), f32[8,4,128]{2,0,1:T(8,128)}) %reduce-scatter.2.cloned.1.call-update) | async-done | bytes 16400 | tf_op jit(solution)/shard_map/reduce_scatter | solution.py:103
  233.7 1.4 fusion.22
  235.1 1.4 fusion.21
  237.4 11.3 %all_to_all.73 = bf16[32,2,256]{2,1,0:T(2,128)(2,1)S(1)} all-to-all(bf16[32,2,256]{2,1,0:T(2,128)(2,1)S(1)} %reshape.329), channel_id=1, replica_groups=mesh['orb'=32,'pln'=16] {'orb'}, dimensions={0} | all-to-all | bytes 65536 | tf_op jit(solution)/shard_map/all_to_all | solution.py:110
  253.7 1.2 copy.153
  255.0 1.7 reshape.331
  256.7 12.3 %all-to-all-start.1 = ((f32[16,1,2048]{2,1,0:T(1,128)}), f32[16,1,2048]{2,1,0:T(1,128)S(1)}, u32[]{:S(2)}, u32[]{:S(2)}) async-start(f32[16,1,2048]{2,1,0:T(1,128)} %reshape.331), calls=%async_computation.2 | async-start | bytes 262144 | tf_op jit(solution)/shard_map/all_to_all | solution.py:114
  269.3 14.4 %all-to-all-done.1 = f32[16,1,2048]{2,1,0:T(1,128)S(1)} async-done(((f32[16,1,2048]{2,1,0:T(1,128)}), f32[16,1,2048]{2,1,0:T(1,128)S(1)}, u32[]{:S(2)}, u32[]{:S(2)}) %all-to-all-start.1) | async-done | bytes 131104 | tf_op jit(solution)/shard_map/all_to_all | solution.py:114
  294.8 18.9 %all_to_all.74 = f32[16,1,2048]{2,1,0:T(1,128)S(1)} all-to-all(f32[16,1,2048]{2,1,0:T(1,128)S(1)} %reshape.333), channel_id=1, replica_groups=mesh['orb'=32,'pln'=16] {'pln'}, dimensions={0} | all-to-all | bytes 262144 | tf_op jit(solution)/shard_map/all_to_all | solution.py:119
  320.3 10.8 %all_to_all.75 = f32[32,1,512]{2,1,0:T(1,128)S(1)} all-to-all(f32[32,1,512]{2,1,0:T(1,128)S(1)} %reshape.335), channel_id=1, replica_groups=mesh['orb'=32,'pln'=16] {'orb'}, dimensions={0} | all-to-all | bytes 131072 | tf_op jit(solution)/shard_map/all_to_all | solution.py:121
  335.3 24.1 %all_gather.6 = f32[8,128,128]{2,0,1:T(8,128)S(1)} all-gather(f32[8,4,128]{2,0,1:T(8,128)S(1)} %copy.170), channel_id=1, replica_groups=mesh['orb'=32,'pln'=16] {'orb'}, dimensions={1}, use_global_device_ids=true | all-gather | bytes 540672 | tf_op jit(solution)/shard_map/all_gather | solution.py:127
  360.3 5.9 %copy.139 = bf16[16,32,32,32]{3,1,2,0:T(8,128)(2,1)} copy(bf16[16,32,32,32]{3,2,1,0:T(8,128)(2,1)} %reshape.255) | data formatting | bytes 2097152 | tf_op jit(solution)/shard_map/reshape | solution.py:89
  372.4 1.4 fusion.31
  375.0 82.4 %all-gather.2.cloned.1.call-done = f32[128,128,128]{2,1,0:T(8,128)} async-done(((f32[8,128,128]{2,1,0:T(8,128)}), f32[128,128,128]{2,1,0:T(8,128)}) %all-gather.2.cloned.1.call-update) | async-done | bytes 8388624 | tf_op jit(solution)/shard_map/all_gather | solution.py:128
  457.4 2.2 convolution_multiply_fusion
  459.5 2.6 fusion.108
  465.8 21.4 %all_to_all.76 = bf16[16,2,1024]{2,1,0:T(2,128)(2,1)S(1)} all-to-all(bf16[16,2,1024]{2,1,0:T(2,128)(2,1)S(1)} %reshape.337), channel_id=1, replica_groups=mesh['orb'=32,'pln'=16] {'pln'}, dimensions={0} | all-to-all | bytes 131072 | tf_op jit(solution)/shard_map/all_to_all | solution.py:145
  (106 shorter events, 37.0 us)
Async XLA Ops:
  6.5 6.8 %copy-start.4 = (s32[2]{0:T(128)S(1)}, s32[2]{0:T(128)}, u32[]{:S(2)}) copy-start(s32[2]{0:T(128)} %constant.68) | copy-start | bytes 28
  6.5 7.1 %copy-start.2 = (f32[16]{0:T(128)S(1)}, f32[16]{0:T(128)}, u32[]{:S(2)}) copy-start(f32[16]{0:T(128)} %constant.63.clone) | copy-start | bytes 196
  6.5 227.2 %reduce-scatter.2.cloned.1.call-start = ((), (), s32[]{:S(2)}) async-start(), calls=%async_computation.6 | async-start | bytes 540672 | tf_op jit(solution)/shard_map/reduce_scatter | solution.py:103
  14.2 8.7 %copy-start.3 = (f32[16]{0:T(128)S(1)}, f32[16]{0:T(128)}, u32[]{:S(2)}) copy-start(f32[16]{0:T(128)} %param.7) | copy-start | bytes 196
  250.4 18.8 %copy-start = (f32[256,16,8]{0,2,1:T(8,128)S(1)}, f32[256,16,8]{0,2,1:T(8,128)}, u32[]{:S(2)}) copy-start(f32[256,16,8]{0,2,1:T(8,128)} %param.9) | copy-start | bytes 393220
  256.7 27.0 %all-to-all-start.1 = ((f32[16,1,2048]{2,1,0:T(1,128)}), f32[16,1,2048]{2,1,0:T(1,128)S(1)}, u32[]{:S(2)}, u32[]{:S(2)}) async-start(f32[16,1,2048]{2,1,0:T(1,128)} %reshape.331), calls=%async_computation.2 | async-start | bytes 262144 | tf_op jit(solution)/shard_map/all_to_all | solution.py:114
  269.0 188.4 %all-gather.2.cloned.1.call-start = ((), (), s32[]{:S(2)}) async-start(), calls=%async_computation.7 | async-start | bytes 8912896 | tf_op jit(solution)/shard_map/all_gather | solution.py:128
  360.3 5.9 %copy-start.1 = (s32[16,3]{0,1:T(4,128)S(1)}, s32[16,3]{0,1:T(4,128)}, u32[]{:S(2)}) copy-start(s32[16,3]{0,1:T(4,128)} %param.8) | copy-start | bytes 580
Sparse Core Ops, SparseCore 0:
  129.1 104.5 reduce-scatter.1
  360.5 96.8 all-gather.1
where the time goes:
time: 504 us; the launch traced here: 495 us
  waiting for transfers between devices  202 us (40%)
  other arithmetic  96.2 us (19%)
  blocking collectives  86.5 us (17%)
  local copies, waits for them, and re-layouts  41.4 us (8%)
  matrix products  37 us (7%)
  between operations  20 us (4%)
  starting transfers between devices  12.5 us (2%)
    reduce_scatter x1, waiting for transfers between devices, per_device(): lax.psum_scatter(partial_density, 'orb', scatter_dimension=1, tiled=True)  105 us
    unnamed x5, other arithmetic  92.6 us
    all_gather x1, waiting for transfers between devices, per_device(): potential_whole = lax.all_gather(potential_slab, 'pln', axis=0, tiled=True)  82.4 us
    all_gather x1, blocking collectives, per_device(): potential_slab = lax.all_gather(potential_rows, 'orb', axis=1, tiled=True)  24.1 us
    all_to_all x1, blocking collectives, per_device(): lax.all_to_all(finished, 'pln', split_axis=1, concat_axis=0, tiled=True)  21.4 us
    all_to_all x1, blocking collectives, per_device(): lax.all_to_all(spectrum, 'pln', split_axis=1, concat_axis=2, tiled=True)  18.9 us
    all_to_all x1, waiting for transfers between devices, per_device(): lax.all_to_all(spectrum, 'pln', split_axis=2, concat_axis=1, tiled=True)  14.4 us
    all_to_all x1, starting transfers between devices, per_device(): lax.all_to_all(spectrum, 'pln', split_axis=2, concat_axis=1, tiled=True)  12.3 us
  transfers between devices with their start and end apart: 3, of which 3 were waited for; matrix products, arithmetic and copies ran while one was open for 2% of the time, Pallas kernels for 0%

commit v1 on v0

v1 whole, which is shorter than its diff:
```python
import math

import jax
import jax.numpy as jnp
import numpy as np
from jax import lax
from jax.experimental import pallas as pl
from jax.experimental.pallas import tpu as pltpu
from jax.sharding import PartitionSpec as P

G = 128
BOX = 32
M = 256
N_ORB = 32
N_PLN = 16
BF = jnp.bfloat16
F32 = jnp.float32

MAGIC_TAPS = (
    8.433424733352934e-07,
    -1.290557201342061e-05,
    8.76298447621056e-05,
    -0.00030158038132690465,
    0.001747237136729939,
    -0.009420470302010804,
    0.023738214637249424,
    0.0612625895831208,
    0.9940415697834004,
    -0.06048952891969835,
    -0.021030251609303816,
    0.013372634148547948,
    -0.0034412814449349387,
    0.0004944322768868992,
    -5.185986881173433e-05,
    2.7273449291197967e-06,
)


def split(values):
    high = np.asarray(values, np.float32).astype(BF)
    low = (np.asarray(values, np.float32) - high.astype(np.float32)).astype(BF)
    return np.stack([high, low])


def tables():
    taps = np.asarray(MAGIC_TAPS, np.float32)
    magic = np.zeros((BOX, BOX), np.float32)
    for i in range(BOX):
        for k in range(BOX):
            if -8 <= k - i <= 7:
                magic[i, k] = taps[k - i + 8]
    depth = np.zeros((G, BOX * N_PLN), np.float32)
    depth[32 : 32 + BOX] = np.repeat(magic, N_PLN, axis=1)
    angle = 2.0 * math.pi * (np.outer(np.arange(M), np.arange(G)) % M) / M
    hartley = np.cos(angle) + np.sin(angle)
    inner = np.tile(magic.T, (1, BOX)).astype(np.float32)
    outer = np.repeat(magic.T, BOX, axis=1).astype(np.float32)
    back = np.concatenate([magic[:, 0::2].T, magic[:, 1::2].T])
    return split(depth), split(hartley), split(hartley.T), inner, outer, split(back), float(magic[0, 0]) ** 2


def dg(a, b, ca, cb):
    return lax.dot_general(a, b, (((ca,), (cb,)), ((), ())), preferred_element_type=F32)


def halves(a):
    high = a.astype(BF)
    return high, (a - high.astype(F32)).astype(BF)


def dot3(a, bh, bl, ca, cb):
    ah, al = halves(a)
    return dg(ah, bh, ca, cb) + (dg(al, bh, ca, cb) + dg(ah, bl, ca, cb))


def dot3r(ah, al, b, ca, cb):
    bh, bl = halves(b)
    return dg(ah, bh, ca, cb) + (dg(al, bh, ca, cb) + dg(ah, bl, ca, cb))


def kernel(
    main,
    orb_ref, occ_ref, off_ref, ker_ref, depth_ref, har_ref, hart_ref, inner_ref, outer_ref, back_ref,
    out_ref,
    x_s, kt_s, psq_s, own_s, q_s, d_s, s1, r1, tr_s, s2, r2, s3, r3, w_s, r4, s5, r5, fs_s, s6, r6, gs_s, kp_s,
    send_sem, rs1, rs2, rs3, rs4, rs5, rs6,
):
    o = lax.axis_index("orb")
    p = lax.axis_index("pln")
    barrier = pltpu.get_barrier_semaphore()

    def greet(axis, me, count):
        def step(d, carry):
            pl.semaphore_signal(
                barrier, inc=1, device_id={axis: lax.rem(me + d, count)}, device_id_type=pl.DeviceIdType.MESH
            )
            return carry

        lax.fori_loop(1, count, step, 0)

    greet("orb", o, N_ORB)
    greet("pln", p, N_PLN)

    def copy_to(axis, src, dst, recv, slot, other, sem_slot):
        return pltpu.make_async_remote_copy(
            src_ref=src, dst_ref=dst, send_sem=send_sem.at[sem_slot], recv_sem=recv.at[slot],
            device_id={axis: other}, device_id_type=pl.DeviceIdType.MESH,
        )

    def send_all(axis, me, count, src_of, dst, recv):
        def step(d, carry):
            other = lax.rem(me + d, count)
            copy_to(axis, src_of(other), dst.at[me], recv, me, other, d).start()
            return carry

        lax.fori_loop(1, count, step, 0)

    def wait_all(axis, me, count, src_of, dst, recv, each=None):
        def step(d, carry):
            other = lax.rem(me + d, count)
            copy_to(axis, src_of(other), dst.at[other], recv, other, other, d).wait()
            return carry

        lax.fori_loop(1, count, step, 0)

    for k in range(BOX):
        x_s[k * 16 : (k + 1) * 16, :] = orb_ref[:, k * 1024 : (k + 1) * 1024]
    col1024 = lax.broadcasted_iota(jnp.int32, (BOX, 1024), 1)
    row32 = lax.broadcasted_iota(jnp.int32, (BOX, 1024), 0)
    inner = inner_ref[...]

    def make_kt(q, carry):
        block = inner * outer_ref[pl.ds(q, 1), :]
        block = jnp.where(col1024 == row32 + q * BOX, 0.0, block)
        kt_s[pl.ds(pl.multiple_of(q * BOX, BOX), BOX), :] = block.astype(BF)
        return carry

    lax.fori_loop(0, BOX, make_kt, 0)

    lane = lax.broadcasted_iota(jnp.int32, (8, 128), 1)
    row8 = lax.broadcasted_iota(jnp.int32, (8, 128), 0)
    hot = jnp.concatenate(
        [jnp.where(lane == row8 + (8 * p - off_ref[n, 0] + 32), 1.0, 0.0) for n in range(N_PLN)], axis=0
    ).astype(BF)
    same = (
        lax.broadcasted_iota(jnp.int32, (128, 512), 0) // 8 == lax.broadcasted_iota(jnp.int32, (128, 512), 1) % N_PLN
    )
    eh = jnp.where(same, dg(hot, depth_ref[0], 1, 0), 0.0).astype(BF)
    el = jnp.where(same, dg(hot, depth_ref[1], 1, 0), 0.0).astype(BF)
    x = x_s[...]
    s = dg(eh, x, 1, 0) + dg(el, x, 1, 0)
    psi = main * s + dg(s.astype(BF), kt_s[...], 1, 0)
    psq_s[...] = psi * psi


    def place(n, carry):
        weight = occ_ref[n]
        ox = off_ref[n, 2]
        inside = (lane >= ox) & (lane < ox + BOX)
        for bt in range(8):
            v = psq_s[pl.ds(pl.multiple_of(n * 8, 8), 8), bt * 128 : (bt + 1) * 128] * weight
            for j in range(4):
                turned = pltpu.roll(v, lax.rem(ox + 128 - 32 * j, 128), 1)
                at = pl.multiple_of((n * BOX + bt * 4 + j) * 8, 8)
                q_s[pl.ds(at, 8), :] = jnp.where(inside, turned, 0.0)
        return carry

    lax.fori_loop(0, N_PLN, place, 0)

    lane_n = lax.broadcasted_iota(jnp.int32, (1, 512), 1)
    oy = jnp.zeros((1, 512), jnp.int32)
    for n in range(N_PLN):
        oy = jnp.where(lane_n // BOX == n, off_ref[n, 1], oy)
    target = oy + lane_n % BOX
    spots = jnp.where(lax.broadcasted_iota(jnp.int32, (G, 512), 0) == target, 1.0, 0.0).astype(BF)
    hh, hl = har_ref[0], har_ref[1]

    def plane(z, carry):
        qz = q_s[pl.ds(z, 512, stride=8), :]
        qh, ql = halves(qz)
        a = dg(spots, qh, 1, 0) + dg(spots, ql, 1, 0)
        d_s[pl.ds(z, 256, stride=8), :] = dot3r(hh, hl, a, 1, 1)
        return carry

    lax.fori_loop(0, 8, plane, 0)
    s1[...] = d_s[...].reshape(N_ORB, 64, 128).astype(BF)

    pl.semaphore_wait(barrier, N_ORB - 1 + N_PLN - 1)
    send_all("orb", o, N_ORB, lambda i: s1.at[i], r1, rs1)

    lane_own = lax.broadcasted_iota(jnp.int32, (BOX, 512), 1) % N_PLN
    oh = jnp.where(lane_own == p, depth_ref[0, 32 : 32 + BOX, :].astype(F32), 0.0).astype(BF)
    ol = jnp.where(lane_own == p, depth_ref[1, 32 : 32 + BOX, :].astype(F32), 0.0).astype(BF)
    s_own = dg(oh, x_s[...], 1, 0) + dg(ol, x_s[...], 1, 0)
    own_s[...] = main * s_own + dg(s_own.astype(BF), kt_s[...], 1, 0)

    for h in range(2):
        d_s[h * 128 : (h + 1) * 128, :] = ker_ref[:, h * 128 : (h + 1) * 128] * (1.0 / float(M) ** 3)
    for kx in range(8):
        for h in range(2):
            kp_s[kx * 16 : (kx + 1) * 16, h * 128 : (h + 1) * 128] = d_s[pl.ds(h * 128 + kx, 16, stride=8), :]

    wait_all("orb", o, N_ORB, lambda i: s1.at[i], r1, rs1)

    def add(d, total):
        return total + r1[lax.rem(o + d, N_ORB)].astype(F32)

    tr = lax.fori_loop(1, N_ORB, add, s1[o].astype(F32))

    y = dot3(tr, hh, hl, 1, 1)
    for i in range(N_PLN):
        total = jnp.zeros((8, 128), F32)
        for kx in range(8):
            v = y[kx * 8 : (kx + 1) * 8, (i // 8) * 128 : (i // 8) * 128 + 128]
            shift = 16 * (kx - i % 8) % 128
            v = pltpu.roll(v, shift, 1) if shift else v
            total = jnp.where(lane // 16 == kx, v, total)
        s2[i] = total
    send_all("pln", p, N_PLN, lambda i: s2.at[i], r2, rs2)
    r2[p] = s2[p]
    wait_all("pln", p, N_PLN, lambda i: s2.at[i], r2, rs2)

    grid_z = r2[...].reshape(G, 128)
    spectrum = dot3(grid_z.T, hh, hl, 1, 1)
    spectrum = spectrum * kp_s[...]
    back_z = dot3r(hart_ref[0], hart_ref[1], spectrum, 1, 1)
    s3[...] = back_z.reshape(N_PLN, 8, 128)
    send_all("pln", p, N_PLN, lambda i: s3.at[i], r3, rs3)
    r3[p] = s3[p]
    wait_all("pln", p, N_PLN, lambda i: s3.at[i], r3, rs3)

    blocks = []
    for kx in range(8):
        sides = []
        for h in range(2):
            total = jnp.zeros((8, 128), F32)
            for i in range(8):
                v = r3[h * 8 + i]
                shift = 16 * (i - kx) % 128
                v = pltpu.roll(v, shift, 1) if shift else v
                total = jnp.where(lane // 16 == i, v, total)
            sides.append(total)
        blocks.append(jnp.concatenate(sides, axis=1))
    w_s[...] = dot3(jnp.concatenate(blocks, axis=0), hh, hl, 1, 0)
    send_all("orb", o, N_ORB, lambda i: w_s, r4, rs4)
    r4[o] = w_s[...]
    wait_all("orb", o, N_ORB, lambda i: w_s, r4, rs4)

    d_s[...] = r4[...].reshape(N_ORB * 64, 128)

    def plane_back(z, carry):
        wz = d_s[pl.ds(z, 256, stride=8), :]
        vh, vl = halves(dot3(wz.T, hh, hl, 1, 0))
        q_s[pl.ds(z, 512, stride=8), :] = dg(spots, vh, 0, 0) + dg(spots, vl, 0, 0)
        return carry

    lax.fori_loop(0, 8, plane_back, 0)

    def box(n, carry):
        ox = off_ref[n, 2]
        for bt in range(8):
            total = jnp.zeros((8, 128), F32)
            for j in range(4):
                v = q_s[pl.ds(pl.multiple_of((n * BOX + bt * 4 + j) * 8, 8), 8), :]
                v = pltpu.roll(v, lax.rem(128 + 32 * j - ox, 128), 1)
                total = jnp.where(lane // 32 == j, v, total)
            s5[n, :, bt * 128 : (bt + 1) * 128] = total
        return carry

    lax.fori_loop(0, N_PLN, box, 0)
    send_all("pln", p, N_PLN, lambda i: s5.at[i], r5, rs5)
    r5[p] = s5[p]
    wait_all("pln", p, N_PLN, lambda i: s5.at[i], r5, rs5)

    bh, bl = halves(r5[...].reshape(G, 1024))
    cut = jnp.where(
        lax.broadcasted_iota(jnp.int32, (BOX, G), 1) == lax.broadcasted_iota(jnp.int32, (BOX, G), 0) + off_ref[p, 0], 1.0, 0.0
    ).astype(BF)
    v_box = dg(cut, bh, 1, 0) + dg(cut, bl, 1, 0)
    u = v_box * own_s[...]
    u = main * u + dg(u.astype(BF), kt_s[...], 1, 1)
    f = dot3r(back_ref[0], back_ref[1], u, 1, 0)
    for t in range(16):
        part = f[(t // 8) * 16 : (t // 8) * 16 + 16, (t % 8) * 128 : (t % 8) * 128 + 128]
        fs_s[t * 16 : (t + 1) * 16, :] = part
    for i in range(N_PLN):
        s6[i] = fs_s[pl.ds(i, 16, stride=16), :].astype(BF)
    send_all("pln", p, N_PLN, lambda i: s6.at[i], r6, rs6)
    r6[p] = s6[p]
    wait_all("pln", p, N_PLN, lambda i: s6.at[i], r6, rs6)
    gs_s[...] = r6[...].astype(F32).reshape(256, 128)
    for t in range(16):
        out_ref[:, t * 128 : (t + 1) * 128] = gs_s[pl.ds(t, 16, stride=16), :].astype(BF)


def per_device(orbitals, occupations, box_offsets, kernel_spectrum):
    depth, har, hart, inner, outer, back, main = tables()
    ker = kernel_spectrum.transpose(1, 2, 0).reshape(128, M)
    vm = pl.BlockSpec(memory_space=pltpu.VMEM)
    sm = pl.BlockSpec(memory_space=pltpu.SMEM)
    V = pltpu.VMEM
    dma = pltpu.SemaphoreType.DMA

    def body(*refs):
        kernel(main, *refs)

    return pl.pallas_call(
        body,
        out_shape=jax.ShapeDtypeStruct((16, 2048), BF),
        in_specs=[vm, sm, sm] + [vm] * 7,
        out_specs=vm,
        scratch_shapes=[
            V((512, 1024), BF),
            V((1024, 1024), BF),
            V((128, 1024), F32),
            V((32, 1024), F32),
            V((4096, 128), F32),
            V((2048, 128), F32),
            V((32, 64, 128), BF),
            V((32, 64, 128), BF),
            V((64, 128), F32),
            V((16, 8, 128), F32),
            V((16, 8, 128), F32),
            V((16, 8, 128), F32),
            V((16, 8, 128), F32),
            V((64, 128), F32),
            V((32, 64, 128), F32),
            V((16, 8, 1024), F32),
            V((16, 8, 1024), F32),
            V((256, 128), F32),
            V((16, 16, 128), BF),
            V((16, 16, 128), BF),
            V((256, 128), F32),
            V((128, 256), F32),
            dma((32,)), dma((32,)), dma((16,)), dma((16,)), dma((32,)), dma((16,)), dma((16,)),
        ],
        compiler_params=pltpu.CompilerParams(collective_id=0, has_side_effects=True, vmem_limit_bytes=48 << 20),
        name="hartree",
    )(orbitals, occupations, box_offsets, ker, depth, har, hart, inner, outer, back)


def solution(mesh):
    in_specs = (P("orb", None), P("orb"), P("orb", None), P(None, "pln", "orb"))
    out_specs = P("orb", "pln")
    return jax.shard_map(per_device, mesh=mesh, in_specs=in_specs, out_specs=out_specs, check_vma=False)
```

time: 504 us -> 111 us (0.22); the launches traced: 495 us -> 108 us
  waiting for transfers between devices: 202 us -> 0 us
  Pallas kernels: 0 us -> 100 us
  other arithmetic: 96.2 us -> 0 us
  blocking collectives: 86.5 us -> 0 us
  matrix products: 37 us -> 0 us
  local copies, waits for them, and re-layouts: 41.4 us -> 8.12 us
  between operations: 20 us -> 0.02 us
  starting transfers between devices: 12.5 us -> 0 us
    reduce_scatter x1 -> x0, waiting for transfers between devices: 105 us -> none  [per_device(): lax.psum_scatter(partial_density, 'orb', scatter_dimension=1, tiled=True)]
    pallas_call x0 -> x1, Pallas kernels: none -> 100 us  [per_device(): pl.pallas_call(body, out_shape=jax.ShapeDtypeStruct((16, 2048), BF), in_s...]
    unnamed x5 -> x0, other arithmetic: 92.6 us -> none
    all_gather x1 -> x0, waiting for transfers between devices: 82.4 us -> none  [per_device(): potential_whole = lax.all_gather(potential_slab, 'pln', axis=0, tiled=True)]
    all_to_all x4 -> x0, blocking collectives: 62.4 us -> none  [the longest x1 21.4 us: per_device(): lax.all_to_all(finished, 'pln', split_axis=1, concat_axis=0, tiled=True)]
    dot_general x21 -> x0, matrix products: 31.4 us -> none  [the longest x2 6.57 us: expand_all(): jnp.einsum('ojk,okyx->ojyx', depth_filters, coefs, precision=PRECISE)]
    all_gather x1 -> x0, blocking collectives: 24.1 us -> none  [per_device(): potential_slab = lax.all_gather(potential_rows, 'orb', axis=1, tiled=True)]
    all_to_all x1 -> x0, waiting for transfers between devices: 14.4 us -> none  [per_device(): lax.all_to_all(spectrum, 'pln', split_axis=2, concat_axis=1, tiled=True)]
  transfers between devices with their start and end apart: 3 -> 0, of which waited for: 3 -> 0; matrix products, arithmetic and copies ran while one was open for 2% -> 0% of each run, Pallas kernels for 0% -> 0%
where the time goes in v1:
time: 111 us; the launch traced here: 108 us
  Pallas kernels  100 us (90%)
  local copies, waits for them, and re-layouts  8.12 us (7%)
    pallas_call x1, Pallas kernels, per_device(): pl.pallas_call(body, out_shape=jax.ShapeDtypeStruct((16, 2048), BF), in_s...  100 us
    unnamed x20, local copies, waits for them, and re-layouts  8.12 us

profile of v1, /device:TPU:6, one launch (start us, length us, event | category | flops | bytes accessed | tf_op | source)
XLA Modules:
  0.0 108.4 jit_solution(3824131117297012641)
XLA Ops:
  0.0 0.0 copy-start.7
  0.0 0.0 copy-start.8
  0.0 0.8 copy.11.refs_2_
  0.8 0.0 copy-done.7
  0.8 0.0 copy-done.8
  0.8 0.0 copy-start
  0.8 1.2 %copy-done = bf16[16,32768]{1,0:T(8,128)(2,1)S(1)} copy-done((bf16[16,32768]{1,0:T(8,128)(2,1)S(1)}, bf16[16,32768]{1,0:T(8,128)(2,1)}, u32[]{:S(2)}) %copy-start) | copy-done | bytes 1048600
  2.0 0.0 copy-start.1
  2.0 0.9 copy-done.1
  3.0 0.0 copy-start.2
  3.0 0.9 copy-done.2
  3.9 0.0 copy-start.3
  3.9 0.9 copy-done.3
  4.8 0.0 copy-start.4
  4.8 0.9 copy-done.4
  5.7 0.0 copy-start.5
  5.7 0.9 copy-done.5
  6.6 0.0 copy-start.6
  6.6 0.9 copy-done.6
  7.5 100.2 %hartree.1 = bf16[16,2048]{1,0:T(8,128)(2,1)S(1)} custom-call(bf16[16,32768]{1,0:T(8,128)(2,1)S(1)} %copy-done, f32[16]{0:T(128)S(1)} %copy-done.8, s32[16,3]{1,0:T(8,128)S(1)} %copy.11.refs_2_, f32[128,256]{1,0:T(8,128)S(1)} %bitcast.3, bf16[2,128,512]{2,1,0:T(8,128)(2,1)S(1)} %copy-done.1, bf16[2,256,128]{2,1,0:T(8,128)(2,1)S(1)} %copy-done.6, ...), custom_call_target="tpu_custom_call" | custom-call | tf_op jit(solution)/shard_map/hartree/pallas_call | solution.py:307
  107.7 0.6 copy.13
Async XLA Ops:
  0.0 0.8 copy-start.7
  0.0 0.8 copy-start.8
  0.8 1.2 %copy-start = (bf16[16,32768]{1,0:T(8,128)(2,1)S(1)}, bf16[16,32768]{1,0:T(8,128)(2,1)}, u32[]{:S(2)}) copy-start(bf16[16,32768]{1,0:T(8,128)(2,1)} %refs_0_.1) | copy-start | bytes 3145732
  2.0 0.9 copy-start.1
  3.0 0.9 copy-start.2
  3.9 0.9 copy-start.3
  4.8 0.9 copy-start.4
  5.7 0.9 copy-start.5
  6.6 0.9 copy-start.6

commit v2 on v1

--- a/solution.py
+++ b/solution.py
@@ -36,6 +36,12 @@
 )
 
 
+NEAR = sorted(
+    [(a, b) for a in range(4) for b in range(4) if (a, b) != (0, 0)],
+    key=lambda d: min(d[0], 4 - d[0]) + min(d[1], 4 - d[1]),
+)
+
+
 def split(values):
     high = np.asarray(values, np.float32).astype(BF)
     low = (np.asarray(values, np.float32) - high.astype(np.float32)).astype(BF)
@@ -80,10 +86,11 @@
 
 def kernel(
     main,
-    orb_ref, occ_ref, off_ref, ker_ref, depth_ref, har_ref, hart_ref, inner_ref, outer_ref, back_ref,
+    orb_hbm, occ_ref, off_ref, ker_hbm, depth_hbm, har_hbm, hart_hbm, inner_hbm, outer_hbm, back_hbm,
     out_ref,
+    ker_ref, depth_ref, har_ref, hart_ref, inner_ref, outer_ref, back_ref,
     x_s, kt_s, psq_s, own_s, q_s, d_s, s1, r1, tr_s, s2, r2, s3, r3, w_s, r4, s5, r5, fs_s, s6, r6, gs_s, kp_s,
-    send_sem, rs1, rs2, rs3, rs4, rs5, rs6,
+    load_sem, send_sem, rs1, rs2, rs3, rs4, rs5, rs6,
 ):
     o = lax.axis_index("orb")
     p = lax.axis_index("pln")
@@ -101,6 +108,33 @@
     greet("orb", o, N_ORB)
     greet("pln", p, N_PLN)
 
+    pairs = (
+        (depth_hbm, depth_ref), (inner_hbm, inner_ref), (outer_hbm, outer_ref), (har_hbm, har_ref),
+        (ker_hbm, ker_ref), (hart_hbm, hart_ref), (back_hbm, back_ref),
+    )
+    loads = [pltpu.make_async_copy(a, b, load_sem.at[i]) for i, (a, b) in enumerate(pairs)]
+    rows_of = lambda k: pltpu.make_async_copy(
+        orb_hbm.at[:, pl.ds(pl.multiple_of(k * 1024, 1024), 1024)],
+        x_s.at[pl.ds(pl.multiple_of(k * 16, 16), 16), :],
+        load_sem.at[8 + k],
+    )
+
+    def start_rows(k, carry):
+        rows_of(k).start()
+        return carry
+
+    def wait_rows(k, carry):
+        rows_of(k).wait()
+        return carry
+
+    for i in (1, 2, 0):
+        loads[i].start()
+    lax.fori_loop(0, BOX, start_rows, 0)
+    for i in (3, 4, 5, 6):
+        loads[i].start()
+    loads[1].wait()
+    loads[2].wait()
+
     def copy_to(axis, src, dst, recv, slot, other, sem_slot):
         return pltpu.make_async_remote_copy(
             src_ref=src, dst_ref=dst, send_sem=send_sem.at[sem_slot], recv_sem=recv.at[slot],
@@ -123,8 +157,6 @@
 
         lax.fori_loop(1, count, step, 0)
 
-    for k in range(BOX):
-        x_s[k * 16 : (k + 1) * 16, :] = orb_ref[:, k * 1024 : (k + 1) * 1024]
     col1024 = lax.broadcasted_iota(jnp.int32, (BOX, 1024), 1)
     row32 = lax.broadcasted_iota(jnp.int32, (BOX, 1024), 0)
     inner = inner_ref[...]
@@ -140,13 +172,15 @@
     lane = lax.broadcasted_iota(jnp.int32, (8, 128), 1)
     row8 = lax.broadcasted_iota(jnp.int32, (8, 128), 0)
     hot = jnp.concatenate(
-        [jnp.where(lane == row8 + (8 * p - off_ref[n, 0] + 32), 1.0, 0.0) for n in range(N_PLN)], axis=0
+        [jnp.where(lane == row8 + (8 * p - off_ref[0, n] + 32), 1.0, 0.0) for n in range(N_PLN)], axis=0
     ).astype(BF)
+    loads[0].wait()
     same = (
         lax.broadcasted_iota(jnp.int32, (128, 512), 0) // 8 == lax.broadcasted_iota(jnp.int32, (128, 512), 1) % N_PLN
     )
     eh = jnp.where(same, dg(hot, depth_ref[0], 1, 0), 0.0).astype(BF)
     el = jnp.where(same, dg(hot, depth_ref[1], 1, 0), 0.0).astype(BF)
+    lax.fori_loop(0, BOX, wait_rows, 0)
     x = x_s[...]
     s = dg(eh, x, 1, 0) + dg(el, x, 1, 0)
     psi = main * s + dg(s.astype(BF), kt_s[...], 1, 0)
@@ -155,7 +189,7 @@
 
     def place(n, carry):
         weight = occ_ref[n]
-        ox = off_ref[n, 2]
+        ox = off_ref[2, n]
         inside = (lane >= ox) & (lane < ox + BOX)
         for bt in range(8):
             v = psq_s[pl.ds(pl.multiple_of(n * 8, 8), 8), bt * 128 : (bt + 1) * 128] * weight
@@ -170,9 +204,11 @@
     lane_n = lax.broadcasted_iota(jnp.int32, (1, 512), 1)
     oy = jnp.zeros((1, 512), jnp.int32)
     for n in range(N_PLN):
-        oy = jnp.where(lane_n // BOX == n, off_ref[n, 1], oy)
+        oy = jnp.where(lane_n // BOX == n, off_ref[1, n], oy)
     target = oy + lane_n % BOX
     spots = jnp.where(lax.broadcasted_iota(jnp.int32, (G, 512), 0) == target, 1.0, 0.0).astype(BF)
+    for i in (3, 4, 5, 6):
+        loads[i].wait()
     hh, hl = har_ref[0], har_ref[1]
 
     def plane(z, carry):
@@ -242,9 +278,38 @@
             sides.append(total)
         blocks.append(jnp.concatenate(sides, axis=1))
     w_s[...] = dot3(jnp.concatenate(blocks, axis=0), hh, hl, 1, 0)
-    send_all("orb", o, N_ORB, lambda i: w_s, r4, rs4)
+    core = lax.rem(o, 2)
+    cx, cy = o // 8, lax.rem(o // 2, 4)
+    mate = o + 1 - 2 * core
+
+    def peer(step, sign):
+        dx, dy = NEAR[step]
+        return 8 * lax.rem(cx + sign * dx + 4, 4) + 2 * lax.rem(cy + sign * dy + 4, 4) + core
+
+    def gather(step):
+        return copy_to("orb", w_s, r4.at[o], rs4, o, peer(step, 1), step + 1)
+
+    def forward(step):
+        src = peer(step, -1)
+        return copy_to("orb", r4.at[src], r4.at[src], rs4, src, mate, step + 17)
+
+    first = copy_to("orb", w_s, r4.at[o], rs4, o, mate, 0)
+    for step in reversed(range(15)):
+        gather(step).start()
+    first.start()
     r4[o] = w_s[...]
-    wait_all("orb", o, N_ORB, lambda i: w_s, r4, rs4)
+    for step in range(15):
+        src = peer(step, -1)
+        copy_to("orb", w_s, r4.at[src], rs4, src, src, step + 1).wait_recv()
+        forward(step).start()
+    for step in range(15):
+        gather(step).wait_send()
+    for step in range(15):
+        forward(step).wait_send()
+        src = peer(step, -1) + 1 - 2 * core
+        copy_to("orb", w_s, r4.at[src], rs4, src, mate, step + 17).wait_recv()
+    first.wait_send()
+    copy_to("orb", w_s, r4.at[mate], rs4, mate, mate, 0).wait_recv()
 
     d_s[...] = r4[...].reshape(N_ORB * 64, 128)
 
@@ -257,14 +322,21 @@
     lax.fori_loop(0, 8, plane_back, 0)
 
     def box(n, carry):
-        ox = off_ref[n, 2]
+        ox = off_ref[2, n]
+        parts = []
         for bt in range(8):
             total = jnp.zeros((8, 128), F32)
             for j in range(4):
                 v = q_s[pl.ds(pl.multiple_of((n * BOX + bt * 4 + j) * 8, 8), 8), :]
                 v = pltpu.roll(v, lax.rem(128 + 32 * j - ox, 128), 1)
                 total = jnp.where(lane // 32 == j, v, total)
-            s5[n, :, bt * 128 : (bt + 1) * 128] = total
+            parts.append(total)
+        whole = (parts[0] + parts[1] + parts[2] + parts[3]) + (parts[4] + parts[5] + parts[6] + parts[7])
+        mean = jnp.broadcast_to(jnp.sum(whole, axis=1, keepdims=True) * (1.0 / 1024), (8, 128)).astype(BF)
+        level = mean.astype(F32)
+        for bt in range(8):
+            s5[n, :, bt * 128 : (bt + 1) * 128] = (parts[bt] - level).astype(BF)
+        s5[n, :, 1024:1152] = mean
         return carry
 
     lax.fori_loop(0, N_PLN, box, 0)
@@ -272,11 +344,11 @@
     r5[p] = s5[p]
     wait_all("pln", p, N_PLN, lambda i: s5.at[i], r5, rs5)
 
-    bh, bl = halves(r5[...].reshape(G, 1024))
     cut = jnp.where(
-        lax.broadcasted_iota(jnp.int32, (BOX, G), 1) == lax.broadcasted_iota(jnp.int32, (BOX, G), 0) + off_ref[p, 0], 1.0, 0.0
+        lax.broadcasted_iota(jnp.int32, (BOX, G), 1) == lax.broadcasted_iota(jnp.int32, (BOX, G), 0) + off_ref[0, p], 1.0, 0.0
     ).astype(BF)
-    v_box = dg(cut, bh, 1, 0) + dg(cut, bl, 1, 0)
+    picked = dg(cut, r5[...].astype(F32).reshape(G, 1152).astype(BF), 1, 0)
+    v_box = picked[:, :1024] + jnp.concatenate([picked[:, 1024:]] * 8, axis=1)
     u = v_box * own_s[...]
     u = main * u + dg(u.astype(BF), kt_s[...], 1, 1)
     f = dot3r(back_ref[0], back_ref[1], u, 1, 0)
@@ -298,6 +370,7 @@
     ker = kernel_spectrum.transpose(1, 2, 0).reshape(128, M)
     vm = pl.BlockSpec(memory_space=pltpu.VMEM)
     sm = pl.BlockSpec(memory_space=pltpu.SMEM)
+    hbm = pl.BlockSpec(memory_space=pltpu.HBM)
     V = pltpu.VMEM
     dma = pltpu.SemaphoreType.DMA
 
@@ -307,9 +380,11 @@
     return pl.pallas_call(
         body,
         out_shape=jax.ShapeDtypeStruct((16, 2048), BF),
-        in_specs=[vm, sm, sm] + [vm] * 7,
+        in_specs=[hbm, sm, sm] + [hbm] * 7,
         out_specs=vm,
         scratch_shapes=[
+            V((128, M), F32), V(depth.shape, BF), V(har.shape, BF), V(hart.shape, BF),
+            V(inner.shape, F32), V(outer.shape, F32), V(back.shape, BF),
             V((512, 1024), BF),
             V((1024, 1024), BF),
             V((128, 1024), F32),
@@ -325,18 +400,18 @@
             V((16, 8, 128), F32),
             V((64, 128), F32),
             V((32, 64, 128), F32),
-            V((16, 8, 1024), F32),
-            V((16, 8, 1024), F32),
+            V((16, 8, 1152), BF),
+            V((16, 8, 1152), BF),
             V((256, 128), F32),
             V((16, 16, 128), BF),
             V((16, 16, 128), BF),
             V((256, 128), F32),
             V((128, 256), F32),
-            dma((32,)), dma((32,)), dma((16,)), dma((16,)), dma((32,)), dma((16,)), dma((16,)),
+            dma((40,)), dma((32,)), dma((32,)), dma((16,)), dma((16,)), dma((32,)), dma((16,)), dma((16,)),
         ],
-        compiler_params=pltpu.CompilerParams(collective_id=0, has_side_effects=True, vmem_limit_bytes=48 << 20),
+        compiler_params=pltpu.CompilerParams(collective_id=0, has_side_effects=True),
         name="hartree",
-    )(orbitals, occupations, box_offsets, ker, depth, har, hart, inner, outer, back)
+    )(orbitals, occupations, box_offsets.T, ker, depth, har, hart, inner, outer, back)
 
 
 def solution(mesh):

time: 111 us -> 91.8 us (0.83); the launches traced: 108 us -> 90.8 us
  Pallas kernels: 100 us -> 89.3 us
  local copies, waits for them, and re-layouts: 8.12 us -> 1.47 us
    pallas_call x1, Pallas kernels: 100 us -> 89.3 us  [per_device(): pl.pallas_call(body, out_shape=jax.ShapeDtypeStruct((16, 2048), BF), in_s...]
    unnamed x20 -> x1, local copies, waits for them, and re-layouts: 8.12 us -> 1.47 us
where the time goes in v2:
time: 91.8 us; the launch traced here: 90.8 us
  Pallas kernels  89.3 us (97%)
  local copies, waits for them, and re-layouts  1.47 us (2%)
    pallas_call x1, Pallas kernels, per_device(): pl.pallas_call(body, out_shape=jax.ShapeDtypeStruct((16, 2048), BF), in_s...  89.3 us

profile of v2, /device:TPU:6, one launch (start us, length us, event | category | flops | bytes accessed | tf_op | source)
XLA Modules:
  0.0 90.8 jit_solution(6477708687346602557)
XLA Ops:
  0.0 89.3 %hartree.1 = bf16[16,2048]{1,0:T(8,128)(2,1)} custom-call(bf16[16,32768]{1,0:T(8,128)(2,1)} %refs_0_.1, f32[16]{0:T(128)} %refs_1_.1, s32[3,16]{1,0:T(4,128)} %bitcast.5, f32[128,256]{1,0:T(8,128)} %bitcast.4, bf16[2,128,512]{2,1,0:T(8,128)(2,1)} %constant.12.clone.refs_4_, bf16[2,256,128]{2,1,0:T(8,128)(2,1)} %constant.13.clone.refs_5_, ...), custom_call_target="tpu_custom_call" | custom-call | tf_op jit(solution)/shard_map/hartree/pallas_call | solution.py:380
  89.4 1.5 %copy.12 = bf16[16,2048]{1,0:T(8,128)(2,1)} copy(bf16[16,2048]{1,0:T(8,128)(2,1)} %hartree.1) | data formatting | bytes 131072

commit v3 on v2

--- a/solution.py
+++ b/solution.py
@@ -13,6 +13,7 @@
 M = 256
 N_ORB = 32
 N_PLN = 16
+UNROLL = 8
 BF = jnp.bfloat16
 F32 = jnp.float32
 
@@ -36,9 +37,9 @@
 )
 
 
-NEAR = sorted(
-    [(a, b) for a in range(4) for b in range(4) if (a, b) != (0, 0)],
-    key=lambda d: min(d[0], 4 - d[0]) + min(d[1], 4 - d[1]),
+FAR = sorted(
+    [(a, b) for a in range(4) for b in range(4)],
+    key=lambda d: -min(d[0], 4 - d[0]) - min(d[1], 4 - d[1]),
 )
 
 
@@ -89,8 +90,8 @@
     orb_hbm, occ_ref, off_ref, ker_hbm, depth_hbm, har_hbm, hart_hbm, inner_hbm, outer_hbm, back_hbm,
     out_ref,
     ker_ref, depth_ref, har_ref, hart_ref, inner_ref, outer_ref, back_ref,
-    x_s, kt_s, psq_s, own_s, q_s, d_s, s1, r1, tr_s, s2, r2, s3, r3, w_s, r4, s5, r5, fs_s, s6, r6, gs_s, kp_s,
-    load_sem, send_sem, rs1, rs2, rs3, rs4, rs5, rs6,
+    x_s, kt_s, psq_s, own_s, q_s, d_s, s1, r1, m1, mr1, s2, r2, s3, r3, w_s, r4, s5, r5, fs_s, s6, r6, gs_s, kp_s,
+    load_sem, send_sem, rsm, rs1, rs2, rs3, rs4, rs5, rs6,
 ):
     o = lax.axis_index("orb")
     p = lax.axis_index("pln")
@@ -141,21 +142,24 @@
             device_id={axis: other}, device_id_type=pl.DeviceIdType.MESH,
         )
 
+    def far(i):
+        return lax.rem(p + 8 + (1 - 2 * lax.rem(i, 2)) * ((i + 1) // 2), N_PLN)
+
     def send_all(axis, me, count, src_of, dst, recv):
-        def step(d, carry):
-            other = lax.rem(me + d, count)
-            copy_to(axis, src_of(other), dst.at[me], recv, me, other, d).start()
+        def step(i, carry):
+            other = far(i)
+            copy_to(axis, src_of(other), dst.at[me], recv, me, other, i).start()
             return carry
 
-        lax.fori_loop(1, count, step, 0)
-
-    def wait_all(axis, me, count, src_of, dst, recv, each=None):
-        def step(d, carry):
-            other = lax.rem(me + d, count)
-            copy_to(axis, src_of(other), dst.at[other], recv, other, other, d).wait()
+        lax.fori_loop(0, count - 1, step, 0)
+
+    def wait_all(axis, me, count, src_of, dst, recv):
+        def step(i, carry):
+            other = far(count - 2 - i)
+            copy_to(axis, src_of(other), dst.at[other], recv, other, other, i).wait()
             return carry
 
-        lax.fori_loop(1, count, step, 0)
+        lax.fori_loop(0, count - 1, step, 0)
 
     col1024 = lax.broadcasted_iota(jnp.int32, (BOX, 1024), 1)
     row32 = lax.broadcasted_iota(jnp.int32, (BOX, 1024), 0)
@@ -218,11 +222,43 @@
         d_s[pl.ds(z, 256, stride=8), :] = dot3r(hh, hl, a, 1, 1)
         return carry
 
-    lax.fori_loop(0, 8, plane, 0)
-    s1[...] = d_s[...].reshape(N_ORB, 64, 128).astype(BF)
-
-    pl.semaphore_wait(barrier, N_ORB - 1 + N_PLN - 1)
-    send_all("orb", o, N_ORB, lambda i: s1.at[i], r1, rs1)
+    lax.fori_loop(0, 8, plane, 0, unroll=UNROLL)
+
+    core = lax.rem(o, 2)
+    cx, cy = o // 8, lax.rem(o // 2, 4)
+    mate = o + 1 - 2 * core
+    here = o // 2
+
+    def chip(step, sign):
+        dx, dy = FAR[step]
+        return 4 * lax.rem(cx + sign * dx + 4, 4) + lax.rem(cy + sign * dy + 4, 4)
+
+    def block(owner):
+        return d_s[pl.ds(pl.multiple_of(owner * 64, 64), 64), :]
+
+    def to_mate(part):
+        rows = pl.ds(part * 8, 8)
+        return copy_to("orb", m1.at[rows], mr1.at[rows], rsm, part, mate, 30 + part)
+
+    def to_chip(step):
+        return copy_to("orb", s1.at[step], r1.at[here], rs1, here, 2 * chip(step, 1) + core, step)
+
+    def from_chip(step):
+        src = chip(step, -1)
+        return copy_to("orb", s1.at[step], r1.at[src], rs1, src, 2 * src + core, step)
+
+    for step in range(16):
+        m1[step] = block(2 * chip(step, 1) + 1 - core).astype(BF)
+        if step == 7:
+            pl.semaphore_wait(barrier, N_ORB - 1 + N_PLN - 1)
+            to_mate(0).start()
+    to_mate(1).start()
+    for step in range(15):
+        if step % 8 == 0:
+            to_mate(step // 8).wait()
+        s1[step] = (block(2 * chip(step, 1) + core) + mr1[step].astype(F32)).astype(BF)
+        to_chip(step).start()
+    tr = block(o) + mr1[15].astype(F32)
 
     lane_own = lax.broadcasted_iota(jnp.int32, (BOX, 512), 1) % N_PLN
     oh = jnp.where(lane_own == p, depth_ref[0, 32 : 32 + BOX, :].astype(F32), 0.0).astype(BF)
@@ -236,12 +272,9 @@
         for h in range(2):
             kp_s[kx * 16 : (kx + 1) * 16, h * 128 : (h + 1) * 128] = d_s[pl.ds(h * 128 + kx, 16, stride=8), :]
 
-    wait_all("orb", o, N_ORB, lambda i: s1.at[i], r1, rs1)
-
-    def add(d, total):
-        return total + r1[lax.rem(o + d, N_ORB)].astype(F32)
-
-    tr = lax.fori_loop(1, N_ORB, add, s1[o].astype(F32))
+    for step in reversed(range(15)):
+        from_chip(step).wait()
+        tr = tr + r1[chip(step, -1)].astype(F32)
 
     y = dot3(tr, hh, hl, 1, 1)
     for i in range(N_PLN):
@@ -278,38 +311,36 @@
             sides.append(total)
         blocks.append(jnp.concatenate(sides, axis=1))
     w_s[...] = dot3(jnp.concatenate(blocks, axis=0), hh, hl, 1, 0)
-    core = lax.rem(o, 2)
-    cx, cy = o // 8, lax.rem(o // 2, 4)
-    mate = o + 1 - 2 * core
-
-    def peer(step, sign):
-        dx, dy = NEAR[step]
-        return 8 * lax.rem(cx + sign * dx + 4, 4) + 2 * lax.rem(cy + sign * dy + 4, 4) + core
-
     def gather(step):
-        return copy_to("orb", w_s, r4.at[o], rs4, o, peer(step, 1), step + 1)
+        return copy_to("orb", w_s, r4.at[o], rs4, o, 2 * chip(step, 1) + core, step)
+
+    def arrive(step):
+        src = 2 * chip(step, -1) + core
+        return copy_to("orb", w_s, r4.at[src], rs4, src, src, step)
 
     def forward(step):
-        src = peer(step, -1)
-        return copy_to("orb", r4.at[src], r4.at[src], rs4, src, mate, step + 17)
-
-    first = copy_to("orb", w_s, r4.at[o], rs4, o, mate, 0)
-    for step in reversed(range(15)):
+        src = 2 * chip(step, -1) + core
+        return copy_to("orb", r4.at[src], r4.at[src], rs4, src, mate, step + 16)
+
+    def passed(step):
+        src = 2 * chip(step, -1) + 1 - core
+        return copy_to("orb", w_s, r4.at[src], rs4, src, mate, step + 16)
+
+    first = copy_to("orb", w_s, r4.at[o], rs4, o, mate, 15)
+    for step in range(15):
         gather(step).start()
     first.start()
     r4[o] = w_s[...]
-    for step in range(15):
-        src = peer(step, -1)
-        copy_to("orb", w_s, r4.at[src], rs4, src, src, step + 1).wait_recv()
+    for step in reversed(range(15)):
+        arrive(step).wait_recv()
         forward(step).start()
     for step in range(15):
         gather(step).wait_send()
-    for step in range(15):
-        forward(step).wait_send()
-        src = peer(step, -1) + 1 - 2 * core
-        copy_to("orb", w_s, r4.at[src], rs4, src, mate, step + 17).wait_recv()
     first.wait_send()
-    copy_to("orb", w_s, r4.at[mate], rs4, mate, mate, 0).wait_recv()
+    for step in reversed(range(16)):
+        passed(step).wait_recv()
+        if step < 15:
+            forward(step).wait_send()
 
     d_s[...] = r4[...].reshape(N_ORB * 64, 128)
 
@@ -319,9 +350,14 @@
         q_s[pl.ds(z, 512, stride=8), :] = dg(spots, vh, 0, 0) + dg(spots, vl, 0, 0)
         return carry
 
-    lax.fori_loop(0, 8, plane_back, 0)
-
-    def box(n, carry):
+    lax.fori_loop(0, 8, plane_back, 0, unroll=UNROLL)
+
+    def send_box(i):
+        n = far(i)
+        return copy_to("pln", s5.at[n], r5.at[p], rs5, p, n, i)
+
+    def box(i, carry):
+        n = far(i)
         ox = off_ref[2, n]
         parts = []
         for bt in range(8):
@@ -339,8 +375,13 @@
         s5[n, :, 1024:1152] = mean
         return carry
 
-    lax.fori_loop(0, N_PLN, box, 0)
-    send_all("pln", p, N_PLN, lambda i: s5.at[i], r5, rs5)
+    def box_out(i, carry):
+        box(i, carry)
+        send_box(i).start()
+        return carry
+
+    lax.fori_loop(0, N_PLN - 1, box_out, 0)
+    box(N_PLN - 1, 0)
     r5[p] = s5[p]
     wait_all("pln", p, N_PLN, lambda i: s5.at[i], r5, rs5)
 
@@ -391,9 +432,10 @@
             V((32, 1024), F32),
             V((4096, 128), F32),
             V((2048, 128), F32),
-            V((32, 64, 128), BF),
-            V((32, 64, 128), BF),
-            V((64, 128), F32),
+            V((16, 64, 128), BF),
+            V((16, 64, 128), BF),
+            V((16, 64, 128), BF),
+            V((16, 64, 128), BF),
             V((16, 8, 128), F32),
             V((16, 8, 128), F32),
             V((16, 8, 128), F32),
@@ -407,7 +449,7 @@
             V((16, 16, 128), BF),
             V((256, 128), F32),
             V((128, 256), F32),
-            dma((40,)), dma((32,)), dma((32,)), dma((16,)), dma((16,)), dma((32,)), dma((16,)), dma((16,)),
+            dma((40,)), dma((32,)), dma((2,)), dma((16,)), dma((16,)), dma((16,)), dma((32,)), dma((16,)), dma((16,)),
         ],
         compiler_params=pltpu.CompilerParams(collective_id=0, has_side_effects=True),
         name="hartree",

time: 91.8 us -> 79.6 us (0.87)
  Pallas kernels: 89.3 us -> 76.6 us
    pallas_call x1, Pallas kernels: 89.3 us -> 76.6 us  [per_device(): pl.pallas_call(body, out_shape=jax.ShapeDtypeStruct((16, 2048), BF), in_s...]
where the time goes in v3:
time: 79.6 us; the launch traced here: 78.1 us
  Pallas kernels  76.6 us (96%)
  local copies, waits for them, and re-layouts  1.47 us (2%)
    pallas_call x1, Pallas kernels, per_device(): pl.pallas_call(body, out_shape=jax.ShapeDtypeStruct((16, 2048), BF), in_s...  76.6 us

profile of v3, /device:TPU:6, one launch (start us, length us, event | category | flops | bytes accessed | tf_op | source)
XLA Modules:
  0.0 78.1 jit_solution(5208560468041372371)
XLA Ops:
  0.0 76.6 %hartree.1 = bf16[16,2048]{1,0:T(8,128)(2,1)} custom-call(bf16[16,32768]{1,0:T(8,128)(2,1)} %refs_0_.1, f32[16]{0:T(128)} %refs_1_.1, s32[3,16]{1,0:T(4,128)} %bitcast.5, f32[128,256]{1,0:T(8,128)} %bitcast.4, bf16[2,128,512]{2,1,0:T(8,128)(2,1)} %constant.12.clone.refs_4_, bf16[2,256,128]{2,1,0:T(8,128)(2,1)} %constant.13.clone.refs_5_, ...), custom_call_target="tpu_custom_call" | custom-call | tf_op jit(solution)/shard_map/hartree/pallas_call | solution.py:421
  76.6 1.5 %copy.12 = bf16[16,2048]{1,0:T(8,128)(2,1)} copy(bf16[16,2048]{1,0:T(8,128)(2,1)} %hartree.1) | data formatting | bytes 131072

commit v4 on v3

--- a/solution.py
+++ b/solution.py
@@ -13,7 +13,6 @@
 M = 256
 N_ORB = 32
 N_PLN = 16
-UNROLL = 8
 BF = jnp.bfloat16
 F32 = jnp.float32
 
@@ -56,14 +55,14 @@
         for k in range(BOX):
             if -8 <= k - i <= 7:
                 magic[i, k] = taps[k - i + 8]
-    depth = np.zeros((G, BOX * N_PLN), np.float32)
-    depth[32 : 32 + BOX] = np.repeat(magic, N_PLN, axis=1)
+    depth = np.repeat(magic, N_PLN, axis=1)
     angle = 2.0 * math.pi * (np.outer(np.arange(M), np.arange(G)) % M) / M
     hartley = np.cos(angle) + np.sin(angle)
+    cyclic = np.arange(G).reshape(8, N_PLN).T.reshape(-1)
     inner = np.tile(magic.T, (1, BOX)).astype(np.float32)
     outer = np.repeat(magic.T, BOX, axis=1).astype(np.float32)
     back = np.concatenate([magic[:, 0::2].T, magic[:, 1::2].T])
-    return split(depth), split(hartley), split(hartley.T), inner, outer, split(back), float(magic[0, 0]) ** 2
+    return split(depth), split(hartley), split(hartley.T), split(hartley[:, cyclic]), split(hartley.T[cyclic]), inner, outer, split(back), float(magic[0, 0]) ** 2
 
 
 def dg(a, b, ca, cb):
@@ -87,10 +86,10 @@
 
 def kernel(
     main,
-    orb_hbm, occ_ref, off_ref, ker_hbm, depth_hbm, har_hbm, hart_hbm, inner_hbm, outer_hbm, back_hbm,
+    orb_hbm, occ_ref, off_ref, ker_hbm, depth_hbm, har_hbm, hart_hbm, harz_hbm, hartz_hbm, inner_hbm, outer_hbm, back_hbm,
     out_ref,
-    ker_ref, depth_ref, har_ref, hart_ref, inner_ref, outer_ref, back_ref,
-    x_s, kt_s, psq_s, own_s, q_s, d_s, s1, r1, m1, mr1, s2, r2, s3, r3, w_s, r4, s5, r5, fs_s, s6, r6, gs_s, kp_s,
+    ker_ref, depth_ref, har_ref, hart_ref, harz_ref, hartz_ref, inner_ref, outer_ref, back_ref,
+    x_s, kt_s, psq_s, own_s, q_s, oh_s, d_s, s1, r1, m1, mr1, s2, r2, s3, r3, w_s, r4, s5, r5, fs_s, s6, r6, gs_s, kp_s,
     load_sem, send_sem, rsm, rs1, rs2, rs3, rs4, rs5, rs6,
 ):
     o = lax.axis_index("orb")
@@ -111,13 +110,13 @@
 
     pairs = (
         (depth_hbm, depth_ref), (inner_hbm, inner_ref), (outer_hbm, outer_ref), (har_hbm, har_ref),
-        (ker_hbm, ker_ref), (hart_hbm, hart_ref), (back_hbm, back_ref),
+        (ker_hbm, ker_ref), (hart_hbm, hart_ref), (back_hbm, back_ref), (harz_hbm, harz_ref), (hartz_hbm, hartz_ref),
     )
     loads = [pltpu.make_async_copy(a, b, load_sem.at[i]) for i, (a, b) in enumerate(pairs)]
     rows_of = lambda k: pltpu.make_async_copy(
         orb_hbm.at[:, pl.ds(pl.multiple_of(k * 1024, 1024), 1024)],
         x_s.at[pl.ds(pl.multiple_of(k * 16, 16), 16), :],
-        load_sem.at[8 + k],
+        load_sem.at[12 + k],
     )
 
     def start_rows(k, carry):
@@ -131,7 +130,7 @@
     for i in (1, 2, 0):
         loads[i].start()
     lax.fori_loop(0, BOX, start_rows, 0)
-    for i in (3, 4, 5, 6):
+    for i in range(3, 9):
         loads[i].start()
     loads[1].wait()
     loads[2].wait()
@@ -174,55 +173,56 @@
     lax.fori_loop(0, BOX, make_kt, 0)
 
     lane = lax.broadcasted_iota(jnp.int32, (8, 128), 1)
-    row8 = lax.broadcasted_iota(jnp.int32, (8, 128), 0)
-    hot = jnp.concatenate(
-        [jnp.where(lane == row8 + (8 * p - off_ref[0, n] + 32), 1.0, 0.0) for n in range(N_PLN)], axis=0
-    ).astype(BF)
+    row = lax.broadcasted_iota(jnp.int32, (BOX, BOX), 0)
+    col = lax.broadcasted_iota(jnp.int32, (BOX, BOX), 1)
+    first_plane = jnp.zeros((BOX, BOX), jnp.int32)
+    for n in range(N_PLN):
+        first_plane = jnp.where(row // 2 == n, (p - off_ref[0, n] + 128) & 15, first_plane)
+    hot = jnp.where(col == first_plane + 16 * (row % 2), 1.0, 0.0).astype(BF)
     loads[0].wait()
-    same = (
-        lax.broadcasted_iota(jnp.int32, (128, 512), 0) // 8 == lax.broadcasted_iota(jnp.int32, (128, 512), 1) % N_PLN
-    )
+    lane512 = lax.broadcasted_iota(jnp.int32, (BOX, 512), 1) % N_PLN
+    same = lax.broadcasted_iota(jnp.int32, (BOX, 512), 0) // 2 == lane512
     eh = jnp.where(same, dg(hot, depth_ref[0], 1, 0), 0.0).astype(BF)
     el = jnp.where(same, dg(hot, depth_ref[1], 1, 0), 0.0).astype(BF)
     lax.fori_loop(0, BOX, wait_rows, 0)
     x = x_s[...]
     s = dg(eh, x, 1, 0) + dg(el, x, 1, 0)
     psi = main * s + dg(s.astype(BF), kt_s[...], 1, 0)
-    psq_s[...] = psi * psi
-
+    psi = psi * psi
+    for t in range(8):
+        psq_s[t * BOX : (t + 1) * BOX, :] = psi[:, t * 128 : (t + 1) * 128]
+
+    pattern = lax.broadcasted_iota(jnp.int32, (BOX, 1024), 0)
+    pattern = 4 * (pattern % 8) + pattern // 8
 
     def place(n, carry):
         weight = occ_ref[n]
         ox = off_ref[2, n]
+        oz = off_ref[0, n]
         inside = (lane >= ox) & (lane < ox + BOX)
-        for bt in range(8):
-            v = psq_s[pl.ds(pl.multiple_of(n * 8, 8), 8), bt * 128 : (bt + 1) * 128] * weight
+        plane = (oz + ((p - oz + 128) & 15) - p) >> 4
+        for h in range(2):
+            v = psq_s[pl.ds(n * 2 + h, 8, stride=BOX), :] * weight
             for j in range(4):
                 turned = pltpu.roll(v, lax.rem(ox + 128 - 32 * j, 128), 1)
-                at = pl.multiple_of((n * BOX + bt * 4 + j) * 8, 8)
+                at = pl.multiple_of(((n * 2 + h) * 4 + j) * 8, 8)
                 q_s[pl.ds(at, 8), :] = jnp.where(inside, turned, 0.0)
+            base = (plane + h) * G + off_ref[1, n]
+            at = pl.multiple_of((n * 2 + h) * BOX, BOX)
+            oh_s[pl.ds(at, BOX), :] = jnp.where(col1024 == pattern + base, 1.0, 0.0).astype(BF)
         return carry
 
     lax.fori_loop(0, N_PLN, place, 0)
 
-    lane_n = lax.broadcasted_iota(jnp.int32, (1, 512), 1)
-    oy = jnp.zeros((1, 512), jnp.int32)
-    for n in range(N_PLN):
-        oy = jnp.where(lane_n // BOX == n, off_ref[1, n], oy)
-    target = oy + lane_n % BOX
-    spots = jnp.where(lax.broadcasted_iota(jnp.int32, (G, 512), 0) == target, 1.0, 0.0).astype(BF)
-    for i in (3, 4, 5, 6):
+    for i in range(3, 9):
         loads[i].wait()
     hh, hl = har_ref[0], har_ref[1]
-
-    def plane(z, carry):
-        qz = q_s[pl.ds(z, 512, stride=8), :]
-        qh, ql = halves(qz)
-        a = dg(spots, qh, 1, 0) + dg(spots, ql, 1, 0)
-        d_s[pl.ds(z, 256, stride=8), :] = dot3r(hh, hl, a, 1, 1)
-        return carry
-
-    lax.fori_loop(0, 8, plane, 0, unroll=UNROLL)
+    qh, ql = halves(q_s[...])
+    both = dg(jnp.concatenate([qh, ql], axis=1), oh_s[...], 0, 0)
+    planes = both[:G] + both[G:]
+    d = dot3r(hh, hl, planes, 1, 0)
+    for z in range(8):
+        d_s[pl.ds(z, 256, stride=8), :] = d[:, z * 128 : (z + 1) * 128]
 
     core = lax.rem(o, 2)
     cx, cy = o // 8, lax.rem(o // 2, 4)
@@ -260,9 +260,12 @@
         to_chip(step).start()
     tr = block(o) + mr1[15].astype(F32)
 
-    lane_own = lax.broadcasted_iota(jnp.int32, (BOX, 512), 1) % N_PLN
-    oh = jnp.where(lane_own == p, depth_ref[0, 32 : 32 + BOX, :].astype(F32), 0.0).astype(BF)
-    ol = jnp.where(lane_own == p, depth_ref[1, 32 : 32 + BOX, :].astype(F32), 0.0).astype(BF)
+    oz_own = off_ref[0, p]
+    own_hot = jnp.where(col == ((row // 2 - oz_own + 128) & 15) + 16 * (row % 2), 1.0, 0.0).astype(BF)
+    oh = jnp.where(lane512 == p, dg(own_hot, depth_ref[0], 1, 0), 0.0).astype(BF)
+    ol = jnp.where(lane512 == p, dg(own_hot, depth_ref[1], 1, 0), 0.0).astype(BF)
+    back_h = dg(back_ref[0], own_hot, 1, 1).astype(BF)
+    back_l = dg(back_ref[1], own_hot, 1, 1).astype(BF)
     s_own = dg(oh, x_s[...], 1, 0) + dg(ol, x_s[...], 1, 0)
     own_s[...] = main * s_own + dg(s_own.astype(BF), kt_s[...], 1, 0)
 
@@ -290,9 +293,9 @@
     wait_all("pln", p, N_PLN, lambda i: s2.at[i], r2, rs2)
 
     grid_z = r2[...].reshape(G, 128)
-    spectrum = dot3(grid_z.T, hh, hl, 1, 1)
+    spectrum = dot3(grid_z.T, harz_ref[0], harz_ref[1], 1, 1)
     spectrum = spectrum * kp_s[...]
-    back_z = dot3r(hart_ref[0], hart_ref[1], spectrum, 1, 1)
+    back_z = dot3r(hartz_ref[0], hartz_ref[1], spectrum, 1, 1)
     s3[...] = back_z.reshape(N_PLN, 8, 128)
     send_all("pln", p, N_PLN, lambda i: s3.at[i], r3, rs3)
     r3[p] = s3[p]
@@ -344,55 +347,49 @@
 
     d_s[...] = r4[...].reshape(N_ORB * 64, 128)
 
-    def plane_back(z, carry):
-        wz = d_s[pl.ds(z, 256, stride=8), :]
-        vh, vl = halves(dot3(wz.T, hh, hl, 1, 0))
-        q_s[pl.ds(z, 512, stride=8), :] = dg(spots, vh, 0, 0) + dg(spots, vl, 0, 0)
-        return carry
-
-    lax.fori_loop(0, 8, plane_back, 0, unroll=UNROLL)
+    w = jnp.concatenate([d_s[pl.ds(z, 256, stride=8), :] for z in range(8)], axis=1)
+    v = dot3r(hart_ref[0], hart_ref[1], w, 1, 0)
+    vh, vl = halves(v)
+    both = dg(oh_s[...], jnp.concatenate([vh, vl], axis=0), 1, 1)
+    q_s[...] = both[:, :G] + both[:, G:]
+
+    def rows16(i):
+        return pl.ds(pl.multiple_of(i * 16, 16), 16)
 
     def send_box(i):
         n = far(i)
-        return copy_to("pln", s5.at[n], r5.at[p], rs5, p, n, i)
-
-    def box(i, carry):
-        n = far(i)
+        return copy_to("pln", s5.at[rows16(n)], r5.at[rows16(p)], rs5, p, n, i)
+
+    def wait_box(i, carry):
+        n = far(N_PLN - 2 - i)
+        copy_to("pln", s5.at[rows16(n)], r5.at[rows16(n)], rs5, n, n, i).wait()
+        return carry
+
+    def box(n, put):
         ox = off_ref[2, n]
-        parts = []
-        for bt in range(8):
+        for h in range(2):
             total = jnp.zeros((8, 128), F32)
             for j in range(4):
-                v = q_s[pl.ds(pl.multiple_of((n * BOX + bt * 4 + j) * 8, 8), 8), :]
-                v = pltpu.roll(v, lax.rem(128 + 32 * j - ox, 128), 1)
-                total = jnp.where(lane // 32 == j, v, total)
-            parts.append(total)
-        whole = (parts[0] + parts[1] + parts[2] + parts[3]) + (parts[4] + parts[5] + parts[6] + parts[7])
-        mean = jnp.broadcast_to(jnp.sum(whole, axis=1, keepdims=True) * (1.0 / 1024), (8, 128)).astype(BF)
-        level = mean.astype(F32)
-        for bt in range(8):
-            s5[n, :, bt * 128 : (bt + 1) * 128] = (parts[bt] - level).astype(BF)
-        s5[n, :, 1024:1152] = mean
-        return carry
+                u = q_s[pl.ds(pl.multiple_of(((n * 2 + h) * 4 + j) * 8, 8), 8), :]
+                u = pltpu.roll(u, lax.rem(128 + 32 * j - ox, 128), 1)
+                total = jnp.where(lane // 32 == j, u, total)
+            put[pl.ds(pl.multiple_of(n * 16 + h * 8, 8), 8), :] = total
 
     def box_out(i, carry):
-        box(i, carry)
+        box(far(i), s5)
         send_box(i).start()
         return carry
 
     lax.fori_loop(0, N_PLN - 1, box_out, 0)
-    box(N_PLN - 1, 0)
-    r5[p] = s5[p]
-    wait_all("pln", p, N_PLN, lambda i: s5.at[i], r5, rs5)
-
-    cut = jnp.where(
-        lax.broadcasted_iota(jnp.int32, (BOX, G), 1) == lax.broadcasted_iota(jnp.int32, (BOX, G), 0) + off_ref[0, p], 1.0, 0.0
-    ).astype(BF)
-    picked = dg(cut, r5[...].astype(F32).reshape(G, 1152).astype(BF), 1, 0)
-    v_box = picked[:, :1024] + jnp.concatenate([picked[:, 1024:]] * 8, axis=1)
-    u = v_box * own_s[...]
+    box(p, r5)
+    lax.fori_loop(0, N_PLN - 1, wait_box, 0)
+
+    own = own_s[...]
+    u = jnp.concatenate(
+        [r5[pl.ds(t, BOX, stride=8), :] * own[:, t * 128 : (t + 1) * 128] for t in range(8)], axis=1
+    )
     u = main * u + dg(u.astype(BF), kt_s[...], 1, 1)
-    f = dot3r(back_ref[0], back_ref[1], u, 1, 0)
+    f = dot3r(back_h, back_l, u, 1, 0)
     for t in range(16):
         part = f[(t // 8) * 16 : (t // 8) * 16 + 16, (t % 8) * 128 : (t % 8) * 128 + 128]
         fs_s[t * 16 : (t + 1) * 16, :] = part
@@ -407,7 +404,7 @@
 
 
 def per_device(orbitals, occupations, box_offsets, kernel_spectrum):
-    depth, har, hart, inner, outer, back, main = tables()
+    depth, har, hart, harz, hartz, inner, outer, back, main = tables()
     ker = kernel_spectrum.transpose(1, 2, 0).reshape(128, M)
     vm = pl.BlockSpec(memory_space=pltpu.VMEM)
     sm = pl.BlockSpec(memory_space=pltpu.SMEM)
@@ -421,16 +418,17 @@
     return pl.pallas_call(
         body,
         out_shape=jax.ShapeDtypeStruct((16, 2048), BF),
-        in_specs=[hbm, sm, sm] + [hbm] * 7,
+        in_specs=[hbm, sm, sm] + [hbm] * 9,
         out_specs=vm,
         scratch_shapes=[
-            V((128, M), F32), V(depth.shape, BF), V(har.shape, BF), V(hart.shape, BF),
+            V((128, M), F32), V(depth.shape, BF), V(har.shape, BF), V(hart.shape, BF), V(harz.shape, BF), V(hartz.shape, BF),
             V(inner.shape, F32), V(outer.shape, F32), V(back.shape, BF),
             V((512, 1024), BF),
             V((1024, 1024), BF),
-            V((128, 1024), F32),
+            V((256, 128), F32),
             V((32, 1024), F32),
-            V((4096, 128), F32),
+            V((1024, 128), F32),
+            V((1024, 1024), BF),
             V((2048, 128), F32),
             V((16, 64, 128), BF),
             V((16, 64, 128), BF),
@@ -442,18 +440,18 @@
             V((16, 8, 128), F32),
             V((64, 128), F32),
             V((32, 64, 128), F32),
-            V((16, 8, 1152), BF),
-            V((16, 8, 1152), BF),
+            V((256, 128), F32),
+            V((256, 128), F32),
             V((256, 128), F32),
             V((16, 16, 128), BF),
             V((16, 16, 128), BF),
             V((256, 128), F32),
             V((128, 256), F32),
-            dma((40,)), dma((32,)), dma((2,)), dma((16,)), dma((16,)), dma((16,)), dma((32,)), dma((16,)), dma((16,)),
+            dma((44,)), dma((32,)), dma((2,)), dma((16,)), dma((16,)), dma((16,)), dma((32,)), dma((16,)), dma((16,)),
         ],
         compiler_params=pltpu.CompilerParams(collective_id=0, has_side_effects=True),
         name="hartree",
-    )(orbitals, occupations, box_offsets.T, ker, depth, har, hart, inner, outer, back)
+    )(orbitals, occupations, box_offsets.T, ker, depth, har, hart, harz, hartz, inner, outer, back)
 
 
 def solution(mesh):

time: 79.6 us -> 71 us (0.89); the launches traced: 78.1 us -> 70.5 us
  Pallas kernels: 76.6 us -> 69 us
    pallas_call x1, Pallas kernels: 76.6 us -> 69 us  [per_device(): pl.pallas_call(body, out_shape=jax.ShapeDtypeStruct((16, 2048), BF), in_s...]
where the time goes in v4:
time: 71 us; the launch traced here: 70.5 us
  Pallas kernels  69 us (97%)
  local copies, waits for them, and re-layouts  1.47 us (2%)
    pallas_call x1, Pallas kernels, per_device(): pl.pallas_call(body, out_shape=jax.ShapeDtypeStruct((16, 2048), BF), in_s...  69 us
    unnamed x1, local copies, waits for them, and re-layouts  1.47 us

profile of v4, /device:TPU:6, one launch (start us, length us, event | category | flops | bytes accessed | tf_op | source)
XLA Modules:
  0.0 70.5 jit_solution(6378848542124442871)
XLA Ops:
  0.0 69.0 %hartree.1 = bf16[16,2048]{1,0:T(8,128)(2,1)} custom-call(bf16[16,32768]{1,0:T(8,128)(2,1)} %refs_0_.1, f32[16]{0:T(128)} %refs_1_.1, s32[3,16]{1,0:T(4,128)} %bitcast.5, f32[128,256]{1,0:T(8,128)} %bitcast.4, bf16[2,32,512]{2,1,0:T(8,128)(2,1)} %constant.16.clone.refs_4_, bf16[2,256,128]{2,1,0:T(8,128)(2,1)} %constant.17.clone.refs_5_, ...), custom_call_target="tpu_custom_call" | custom-call | tf_op jit(solution)/shard_map/hartree/pallas_call | solution.py:418
  69.0 1.5 %copy.14 = bf16[16,2048]{1,0:T(8,128)(2,1)} copy(bf16[16,2048]{1,0:T(8,128)(2,1)} %hartree.1) | data formatting | bytes 131072

commit v5 on v4

--- a/solution.py
+++ b/solution.py
@@ -162,15 +162,30 @@
 
     col1024 = lax.broadcasted_iota(jnp.int32, (BOX, 1024), 1)
     row32 = lax.broadcasted_iota(jnp.int32, (BOX, 1024), 0)
-    inner = inner_ref[...]
-
-    def make_kt(q, carry):
-        block = inner * outer_ref[pl.ds(q, 1), :]
-        block = jnp.where(col1024 == row32 + q * BOX, 0.0, block)
-        kt_s[pl.ds(pl.multiple_of(q * BOX, BOX), BOX), :] = block.astype(BF)
-        return carry
-
-    lax.fori_loop(0, BOX, make_kt, 0)
+    def reach(i):
+        return max(i - 1, 0) * 256, min(i + 2, 4) * 256
+
+    for i in range(4):
+        lo, hi = reach(i)
+        inner = inner_ref[:, lo:hi]
+        spot = col1024[:, lo:hi] - row32[:, lo:hi]
+
+        def make_kt(q, carry, lo=lo, hi=hi, inner=inner, spot=spot):
+            block = jnp.where(spot == q * BOX, 0.0, inner * outer_ref[pl.ds(q, 1), lo:hi])
+            kt_s[pl.ds(pl.multiple_of(q * BOX, BOX), BOX), lo:hi] = block.astype(BF)
+            return carry
+
+        lax.fori_loop(8 * i, 8 * i + 8, make_kt, 0)
+
+    def filtered(a, back):
+        low = a.astype(BF)
+        parts = []
+        for i in range(4):
+            lo, hi = reach(i)
+            piece = kt_s[i * 256 : i * 256 + 256, lo:hi] if back else kt_s[lo:hi, i * 256 : i * 256 + 256]
+            parts.append(dg(low[:, lo:hi], piece, 1, 1 if back else 0))
+        return main * a + jnp.concatenate(parts, axis=1)
+
 
     lane = lax.broadcasted_iota(jnp.int32, (8, 128), 1)
     row = lax.broadcasted_iota(jnp.int32, (BOX, BOX), 0)
@@ -186,8 +201,8 @@
     el = jnp.where(same, dg(hot, depth_ref[1], 1, 0), 0.0).astype(BF)
     lax.fori_loop(0, BOX, wait_rows, 0)
     x = x_s[...]
-    s = dg(eh, x, 1, 0) + dg(el, x, 1, 0)
-    psi = main * s + dg(s.astype(BF), kt_s[...], 1, 0)
+    s = dg(jnp.concatenate([eh, el], axis=0), x, 1, 0)
+    psi = filtered(s[:BOX] + s[BOX:], False)
     psi = psi * psi
     for t in range(8):
         psq_s[t * BOX : (t + 1) * BOX, :] = psi[:, t * 128 : (t + 1) * 128]
@@ -266,8 +281,8 @@
     ol = jnp.where(lane512 == p, dg(own_hot, depth_ref[1], 1, 0), 0.0).astype(BF)
     back_h = dg(back_ref[0], own_hot, 1, 1).astype(BF)
     back_l = dg(back_ref[1], own_hot, 1, 1).astype(BF)
-    s_own = dg(oh, x_s[...], 1, 0) + dg(ol, x_s[...], 1, 0)
-    own_s[...] = main * s_own + dg(s_own.astype(BF), kt_s[...], 1, 0)
+    s_own = dg(jnp.concatenate([oh, ol], axis=0), x_s[...], 1, 0)
+    own_s[...] = filtered(s_own[:BOX] + s_own[BOX:], False)
 
     for h in range(2):
         d_s[h * 128 : (h + 1) * 128, :] = ker_ref[:, h * 128 : (h + 1) * 128] * (1.0 / float(M) ** 3)
@@ -287,12 +302,12 @@
             shift = 16 * (kx - i % 8) % 128
             v = pltpu.roll(v, shift, 1) if shift else v
             total = jnp.where(lane // 16 == kx, v, total)
-        s2[i] = total
+        s2[i] = total.astype(BF)
     send_all("pln", p, N_PLN, lambda i: s2.at[i], r2, rs2)
     r2[p] = s2[p]
     wait_all("pln", p, N_PLN, lambda i: s2.at[i], r2, rs2)
 
-    grid_z = r2[...].reshape(G, 128)
+    grid_z = r2[...].astype(F32).reshape(G, 128)
     spectrum = dot3(grid_z.T, harz_ref[0], harz_ref[1], 1, 1)
     spectrum = spectrum * kp_s[...]
     back_z = dot3r(hartz_ref[0], hartz_ref[1], spectrum, 1, 1)
@@ -314,26 +329,29 @@
             sides.append(total)
         blocks.append(jnp.concatenate(sides, axis=1))
     w_s[...] = dot3(jnp.concatenate(blocks, axis=0), hh, hl, 1, 0)
+    def rows64(i):
+        return pl.ds(pl.multiple_of(i * 64, 64), 64)
+
     def gather(step):
-        return copy_to("orb", w_s, r4.at[o], rs4, o, 2 * chip(step, 1) + core, step)
+        return copy_to("orb", w_s, r4.at[rows64(o)], rs4, o, 2 * chip(step, 1) + core, step)
 
     def arrive(step):
         src = 2 * chip(step, -1) + core
-        return copy_to("orb", w_s, r4.at[src], rs4, src, src, step)
+        return copy_to("orb", w_s, r4.at[rows64(src)], rs4, src, src, step)
 
     def forward(step):
         src = 2 * chip(step, -1) + core
-        return copy_to("orb", r4.at[src], r4.at[src], rs4, src, mate, step + 16)
+        return copy_to("orb", r4.at[rows64(src)], r4.at[rows64(src)], rs4, src, mate, step + 16)
 
     def passed(step):
         src = 2 * chip(step, -1) + 1 - core
-        return copy_to("orb", w_s, r4.at[src], rs4, src, mate, step + 16)
-
-    first = copy_to("orb", w_s, r4.at[o], rs4, o, mate, 15)
+        return copy_to("orb", w_s, r4.at[rows64(src)], rs4, src, mate, step + 16)
+
+    first = copy_to("orb", w_s, r4.at[rows64(o)], rs4, o, mate, 15)
     for step in range(15):
         gather(step).start()
     first.start()
-    r4[o] = w_s[...]
+    r4[rows64(o), :] = w_s[...]
     for step in reversed(range(15)):
         arrive(step).wait_recv()
         forward(step).start()
@@ -345,9 +363,8 @@
         if step < 15:
             forward(step).wait_send()
 
-    d_s[...] = r4[...].reshape(N_ORB * 64, 128)
-
-    w = jnp.concatenate([d_s[pl.ds(z, 256, stride=8), :] for z in range(8)], axis=1)
+
+    w = jnp.concatenate([r4[pl.ds(z, 256, stride=8), :] for z in range(8)], axis=1)
     v = dot3r(hart_ref[0], hart_ref[1], w, 1, 0)
     vh, vl = halves(v)
     both = dg(oh_s[...], jnp.concatenate([vh, vl], axis=0), 1, 1)
@@ -388,7 +405,7 @@
     u = jnp.concatenate(
         [r5[pl.ds(t, BOX, stride=8), :] * own[:, t * 128 : (t + 1) * 128] for t in range(8)], axis=1
     )
-    u = main * u + dg(u.astype(BF), kt_s[...], 1, 1)
+    u = filtered(u, True)
     f = dot3r(back_h, back_l, u, 1, 0)
     for t in range(16):
         part = f[(t // 8) * 16 : (t // 8) * 16 + 16, (t % 8) * 128 : (t % 8) * 128 + 128]
@@ -417,7 +434,7 @@
 
     return pl.pallas_call(
         body,
-        out_shape=jax.ShapeDtypeStruct((16, 2048), BF),
+        out_shape=pltpu.VMEM((16, 2048), BF),
         in_specs=[hbm, sm, sm] + [hbm] * 9,
         out_specs=vm,
         scratch_shapes=[
@@ -434,12 +451,12 @@
             V((16, 64, 128), BF),
             V((16, 64, 128), BF),
             V((16, 64, 128), BF),
-            V((16, 8, 128), F32),
-            V((16, 8, 128), F32),
+            V((16, 8, 128), BF),
+            V((16, 8, 128), BF),
             V((16, 8, 128), F32),
             V((16, 8, 128), F32),
             V((64, 128), F32),
-            V((32, 64, 128), F32),
+            V((2048, 128), F32),
             V((256, 128), F32),
             V((256, 128), F32),
             V((256, 128), F32),

time: 71 us -> 68.6 us (0.966)
  Pallas kernels: 69 us -> 67.1 us
  local copies, waits for them, and re-layouts: 1.47 us -> 0.63 us
    pallas_call x1, Pallas kernels: 69 us -> 67.1 us  [per_device(): pl.pallas_call(body, out_shape=pltpu.VMEM((16, 2048), BF), in_specs=[hbm,...]
    unnamed x1, local copies, waits for them, and re-layouts: 1.47 us -> 0.63 us
where the time goes in v5:
time: 68.6 us; the launch traced here: 67.8 us
  Pallas kernels  67.1 us (98%)
    pallas_call x1, Pallas kernels, per_device(): pl.pallas_call(body, out_shape=pltpu.VMEM((16, 2048), BF), in_specs=[hbm,...  67.1 us

profile of v5, /device:TPU:6, one launch (start us, length us, event | category | flops | bytes accessed | tf_op | source)
XLA Modules:
  0.0 67.8 jit_solution(16266356031833523605)
XLA Ops:
  0.0 67.1 %hartree.1 = bf16[16,2048]{1,0:T(8,128)(2,1)S(1)} custom-call(bf16[16,32768]{1,0:T(8,128)(2,1)} %refs_0_.1, f32[16]{0:T(128)} %refs_1_.1, s32[3,16]{1,0:T(4,128)} %bitcast.5, f32[128,256]{1,0:T(8,128)} %bitcast.4, bf16[2,32,512]{2,1,0:T(8,128)(2,1)} %constant.16.clone.refs_4_, bf16[2,256,128]{2,1,0:T(8,128)(2,1)} %constant.17.clone.refs_5_, ...), custom_call_target="tpu_custom_call" | custom-call | tf_op jit(solution)/shard_map/hartree/pallas_call | solution.py:435
  67.1 0.6 copy.14

commit v6 on v5

--- a/solution.py
+++ b/solution.py
@@ -89,8 +89,8 @@
     orb_hbm, occ_ref, off_ref, ker_hbm, depth_hbm, har_hbm, hart_hbm, harz_hbm, hartz_hbm, inner_hbm, outer_hbm, back_hbm,
     out_ref,
     ker_ref, depth_ref, har_ref, hart_ref, harz_ref, hartz_ref, inner_ref, outer_ref, back_ref,
-    x_s, kt_s, psq_s, own_s, q_s, oh_s, d_s, s1, r1, m1, mr1, s2, r2, s3, r3, w_s, r4, s5, r5, fs_s, s6, r6, gs_s, kp_s,
-    load_sem, send_sem, rsm, rs1, rs2, rs3, rs4, rs5, rs6,
+    x_s, kt_s, psq_s, own_s, q_s, oh_s, d_s, s1, r1, m1, mr1, s2, r2, s3, r3, w_s, l_s, rl, r4, s5, r5, fs_s, s6, r6, gs_s, kp_s,
+    load_sem, send_sem, rsm, rs1, rs2, rs3, rs4, rsl, rs5, rs6,
 ):
     o = lax.axis_index("orb")
     p = lax.axis_index("pln")
@@ -328,7 +328,9 @@
                 total = jnp.where(lane // 16 == i, v, total)
             sides.append(total)
         blocks.append(jnp.concatenate(sides, axis=1))
-    w_s[...] = dot3(jnp.concatenate(blocks, axis=0), hh, hl, 1, 0)
+    w_high, w_low = halves(dot3(jnp.concatenate(blocks, axis=0), hh, hl, 1, 0))
+    w_s[...] = w_high
+    l_s[...] = w_low
     def rows64(i):
         return pl.ds(pl.multiple_of(i * 64, 64), 64)
 
@@ -347,7 +349,22 @@
         src = 2 * chip(step, -1) + 1 - core
         return copy_to("orb", w_s, r4.at[rows64(src)], rs4, src, mate, step + 16)
 
+    def low_out(step):
+        return copy_to("orb", l_s, rl.at[core], rsl, core, 2 * chip(step, 1) + core, step + 32)
+
+    def low_on(src_ref):
+        return copy_to("orb", src_ref, rl.at[core], rsl, core, mate, 47)
+
     first = copy_to("orb", w_s, r4.at[rows64(o)], rs4, o, mate, 15)
+    lowest = o == 31 * core
+
+    @pl.when(lowest)
+    def _():
+        for step in range(15):
+            low_out(step).start()
+        low_on(l_s).start()
+        rl[core] = l_s[...]
+
     for step in range(15):
         gather(step).start()
     first.start()
@@ -355,6 +372,12 @@
     for step in reversed(range(15)):
         arrive(step).wait_recv()
         forward(step).start()
+
+    @pl.when(jnp.logical_not(lowest))
+    def _():
+        low_out(0).wait_recv()
+        low_on(rl.at[core]).start()
+
     for step in range(15):
         gather(step).wait_send()
     first.wait_send()
@@ -363,8 +386,19 @@
         if step < 15:
             forward(step).wait_send()
 
-
-    w = jnp.concatenate([r4[pl.ds(z, 256, stride=8), :] for z in range(8)], axis=1)
+    @pl.when(lowest)
+    def _():
+        for step in range(15):
+            low_out(step).wait_send()
+
+    low_on(l_s).wait_send()
+    copy_to("orb", l_s, rl.at[1 - core], rsl, 1 - core, mate, 47).wait_recv()
+
+
+    d_s[...] = r4[...].astype(F32)
+    for i in range(2):
+        d_s[i * 1984 : i * 1984 + 64, :] = d_s[i * 1984 : i * 1984 + 64, :] + rl[i].astype(F32)
+    w = jnp.concatenate([d_s[pl.ds(z, 256, stride=8), :] for z in range(8)], axis=1)
     v = dot3r(hart_ref[0], hart_ref[1], w, 1, 0)
     vh, vl = halves(v)
     both = dg(oh_s[...], jnp.concatenate([vh, vl], axis=0), 1, 1)
@@ -455,8 +489,10 @@
             V((16, 8, 128), BF),
             V((16, 8, 128), F32),
             V((16, 8, 128), F32),
-            V((64, 128), F32),
-            V((2048, 128), F32),
+            V((64, 128), BF),
+            V((64, 128), BF),
+            V((2, 64, 128), BF),
+            V((2048, 128), BF),
             V((256, 128), F32),
             V((256, 128), F32),
             V((256, 128), F32),
@@ -464,7 +500,7 @@
             V((16, 16, 128), BF),
             V((256, 128), F32),
             V((128, 256), F32),
-            dma((44,)), dma((32,)), dma((2,)), dma((16,)), dma((16,)), dma((16,)), dma((32,)), dma((16,)), dma((16,)),
+            dma((44,)), dma((48,)), dma((2,)), dma((16,)), dma((16,)), dma((16,)), dma((32,)), dma((2,)), dma((16,)), dma((16,)),
         ],
         compiler_params=pltpu.CompilerParams(collective_id=0, has_side_effects=True),
         name="hartree",

time: 68.6 us -> 67.9 us (0.990)
  no operation moved by 1% of the time
where the time goes in v6:
time: 67.9 us; the launch traced here: 67.5 us
  Pallas kernels  66.8 us (98%)
    pallas_call x1, Pallas kernels, per_device(): pl.pallas_call(body, out_shape=pltpu.VMEM((16, 2048), BF), in_specs=[hbm,...  66.8 us

profile of v6, /device:TPU:6, one launch (start us, length us, event | category | flops | bytes accessed | tf_op | source)
XLA Modules:
  0.0 67.5 jit_solution(11381193809844662336)
XLA Ops:
  0.0 66.8 %hartree.1 = bf16[16,2048]{1,0:T(8,128)(2,1)S(1)} custom-call(bf16[16,32768]{1,0:T(8,128)(2,1)} %refs_0_.1, f32[16]{0:T(128)} %refs_1_.1, s32[3,16]{1,0:T(4,128)} %bitcast.5, f32[128,256]{1,0:T(8,128)} %bitcast.4, bf16[2,32,512]{2,1,0:T(8,128)(2,1)} %constant.16.clone.refs_4_, bf16[2,256,128]{2,1,0:T(8,128)(2,1)} %constant.17.clone.refs_5_, ...), custom_call_target="tpu_custom_call" | custom-call | tf_op jit(solution)/shard_map/hartree/pallas_call | solution.py:469
  66.9 0.6 copy.14
